TPU v7x, 256 devices: a whole 4x4x8 slice. The times are simulated.
256 devices in a mesh: band: 4 (over y_lo, core), tile: 64 (over y_hi, x, z).
Axes of the slice: x: 4, y: 4 (y_hi: 2, y_lo: 2; y = y_hi * 2 + y_lo), z: 8, core: 2. Of those that a mesh axis runs over, the one named last changes fastest.
Arguments:
- sketch: float32 [8, 4, 384, 128, 128], P(None, 'band', 'tile'), may hold values from -6 to 6
- diag_coef: float32 [4, 384, 128], P('band', 'tile'), may hold values from 1 to 2
- couple: float32 [4, 384, 128], P('band', 'tile'), may hold values from 0.3 to 0.8
- kernel: bfloat16 [8, 512, 4, 384, 128], P(None, None, 'band', 'tile'), may hold values from -0.0048828125 to 0.0048828125
- noise_prec: float32 [8, 512], replicated, may hold values from 0.5 to 4
Outputs:
- hessian_sketch: float32 [8, 4, 384, 128, 128], P(None, 'band', 'tile')
All inputs are finite; a program needn't handle non-finite values.
Results may differ from a plain program's by a relative error of at most 0.0041.
Values may be sent and summed in bfloat16 or wider, within the bound.
A program may use at most 128 MiB of HBM per device.

v0:
```python
import jax
import jax.numpy as jnp
from jax import lax
from jax.sharding import PartitionSpec as P


def with_halo(cells, sides, width):
    for axis, dim in sides:
        count = lax.axis_size(axis)
        ends = count - 1
        head = lax.slice_in_dim(cells, 0, width, axis=dim)
        tail = lax.slice_in_dim(cells, cells.shape[dim] - width, cells.shape[dim], axis=dim)
        cells = jnp.concatenate(
            [
                lax.ppermute(tail, axis, [(i, (i + 1) % count) for i in range(ends)]),
                cells,
                lax.ppermute(head, axis, [((i + 1) % count, i) for i in range(ends)]),
            ],
            axis=dim,
        )
    return cells


def cut_along(x, dim, length):
    before, after = (x.shape[:dim], x.shape[dim + 1 :])
    return jnp.moveaxis(x.reshape(*before, length, -1, *after), dim, 0)


def sum_at_owner(x, axis, dim):
    length = lax.axis_size(axis)
    pieces = lax.all_to_all(cut_along(x, dim, length), axis, 0, 0, tiled=True)
    return jnp.sum(pieces, axis=0)


def from_everyone(x, axis):
    copies = jnp.broadcast_to(x, (lax.axis_size(axis), *x.shape))
    return lax.all_to_all(copies, axis, split_axis=0, concat_axis=0, tiled=True)


def over_copies(x, axis):
    return from_everyone(x, axis).sum(axis=0)


def in_order(pieces, dim):
    dims = list(pieces.shape[1:])
    dims[dim] *= pieces.shape[0]
    return jnp.moveaxis(pieces, 0, dim).reshape(dims)


def gather_directly(x, axis, dim):
    return in_order(from_everyone(x, axis), dim)


def column_sum(coupled):
    padded = jnp.pad(coupled, ((0, 0), (0, 0), (0, 0), (1, 1), (0, 0)))
    return padded[:, :, :, 2:] + padded[:, :, :, :-2]


def sweep_rim(field, diag_full, couple_full):
    coupled = couple_full * field
    extended = with_halo(coupled, (("tile", 2),), 1)
    vertical = extended[:, :, 2:] + extended[:, :, :-2]
    return diag_full * field - couple_full * (vertical + column_sum(coupled))


def adjoint_add(total, kern_flat, piece):
    steps = piece.shape[0]
    for lag in range(steps):
        term = jnp.einsum(
            "sp,tsk->tpk", kern_flat[lag], piece[lag:], preferred_element_type=jnp.float32
        )
        total = total.at[: steps - lag].add(term)
    return total


def body(sketch, diag_coef, couple, kernel, noise_prec):
    steps, one, rows, cols, width = sketch.shape
    sensors = kernel.shape[1]
    points = rows * cols
    diag_full = diag_coef[None, :, :, :, None]
    couple_full = couple[None, :, :, :, None]

    def prior(field):
        return sweep_rim(sweep_rim(field, diag_full, couple_full), diag_full, couple_full)

    smoothed = prior(sketch).astype(jnp.bfloat16).reshape(steps, points, width)
    kern_flat = kernel.reshape(steps, sensors, points)
    data = jnp.zeros((steps, sensors, width), jnp.float32)
    for lag in range(steps):
        term = jnp.einsum(
            "sp,tpk->tsk",
            kern_flat[lag],
            smoothed[: steps - lag],
            preferred_element_type=jnp.float32,
        )
        data = data.at[lag:].add(term)
    empty = jnp.zeros((steps, points, width), jnp.float32)
    share = sum_at_owner(data, "tile", 1)
    share = over_copies(share, "band")
    count = share.shape[1]
    prec_rows = lax.dynamic_slice_in_dim(noise_prec, lax.axis_index("tile") * count, count, 1)
    weighted_share = (share * prec_rows[:, :, None]).astype(jnp.bfloat16)
    adjoint = adjoint_add(empty, kern_flat, gather_directly(weighted_share, "tile", 1))
    adjoint = adjoint.reshape(steps, one, rows, cols, width)
    return prior(adjoint)


def solution(mesh):
    placed = (
        P(None, "band", "tile", None, None),
        P("band", "tile", None),
        P("band", "tile", None),
        P(None, None, "band", "tile", None),
        P(),
    )
    return jax.shard_map(
        body,
        mesh=mesh,
        in_specs=placed,
        out_specs=P(None, "band", "tile", None, None),
        check_vma=False,
    )
```

profile of v0, /device:TPU:16, one launch (start us, length us, event | category | flops | bytes accessed | tf_op | source)
XLA Modules:
  0.0 265.8 jit_solution(15622888149714659640)
XLA Ops:
  0.7 2.4 copy.124
  3.5 9.7 %collective-permute-start = (f32[8,1,1,128,128]{3,4,2,1,0:T(8,128)S(1)}, f32[8,1,1,128,128]{3,4,2,1,0:T(8,128)S(1)}, u32[]{:S(2)}, u32[]{:S(2)}) collective-permute-start(f32[8,1,1,128,128]{3,4,2,1,0:T(8,128)S(1)} %get-tuple-element.231), channel_id=1, source_target_pairs={{1,0},{2,1},{3,2},{4,3},{5,4},{6,5},{7,6},{8,7},{9,8},{10,9},{11,1... | collective-permute-start | bytes 1572872 | tf_op jit(solution)/shard_map/ppermute | solution.py:17
  13.2 1.9 collective-permute-start.1
  15.2 9.2 %collective-permute-done = f32[8,1,1,128,128]{3,4,2,1,0:T(8,128)S(1)} collective-permute-done((f32[8,1,1,128,128]{3,4,2,1,0:T(8,128)S(1)}, f32[8,1,1,128,128]{3,4,2,1,0:T(8,128)S(1)}, u32[]{:S(2)}, u32[]{:S(2)}) %collective-permute-start) | collective-permute-done | bytes 524320 | tf_op jit(solution)/shard_map/ppermute | solution.py:17
  24.4 9.8 %collective-permute-done.1 = f32[8,1,1,128,128]{3,4,2,1,0:T(8,128)S(1)} collective-permute-done((f32[8,1,1,128,128]{3,4,2,1,0:T(8,128)S(1)}, f32[8,1,1,128,128]{3,4,2,1,0:T(8,128)S(1)}, u32[]{:S(2)}, u32[]{:S(2)}) %collective-permute-start.1) | collective-permute-done | bytes 524320 | tf_op jit(solution)/shard_map/ppermute | solution.py:15
  34.2 3.0 %broadcast_multiply_fusion.2 = (f32[8,1,6,128,128]{3,4,2,1,0:T(8,128)S(1)}, f32[8,1,6,128,128]{3,4,2,1,0:T(8,128)}) fusion(f32[6,128]{1,0:T(8,128)S(1)} %bitcast.205, f32[8,1,6,128,128]{3,4,2,1,0:T(8,128)S(1)} %broadcast_multiply_fusion.3, f32[8,1,1,128,128]{3,4,2,1,0:T(8,128)S(1)} %collective-permute-done.1, ...), kind=kLoop, calls=%fused_computation.47 | loop fusion | flops 7077888 | bytes 13637632 | tf_op jit(solution)/shard_map/mul | solution.py:60
  37.2 1.7 copy-done.5
  40.0 1.9 collective-permute-start.2
  41.9 3.9 %collective-permute-start.3 = (f32[8,1,1,128,128]{3,4,2,1,0:T(8,128)}, f32[8,1,1,128,128]{3,4,2,1,0:T(8,128)}, u32[]{:S(2)}, u32[]{:S(2)}) collective-permute-start(f32[8,1,1,128,128]{3,4,2,1,0:T(8,128)} %get-tuple-element.230), channel_id=1, source_target_pairs={{0,1},{1,2},{2,3},{3,4},{4,5},{5,6},{6,7},{7,8},{8,9},{9,10},{10,1... | collective-permute-start | bytes 1572872 | tf_op jit(solution)/shard_map/ppermute | solution.py:15
  45.9 2.0 fusion.40
  47.8 1.4 copy.220
  49.3 2.6 copy.221
  51.8 2.3 copy.222
  54.1 2.3 copy.223
  60.0 2.4 collective-permute-done.3
  62.4 7.3 %fusion.8 = bf16[8,1,6,128,128]{3,4,2,1,0:T(8,128)(2,1)S(1)} fusion(f32[8,1,6,128,128]{3,4,2,1,0:T(8,128)} %copy-done.5, f32[8,1,1,128,128]{3,4,2,1,0:T(8,128)} %collective-permute-done.3, f32[8,1,1,128,128]{3,4,2,1,0:T(8,128)} %collective-permute-done.2, f32[8,1,6,128,128]{3,4,2,1,0:T(8,128)} %get-tuple-element.216, f32[6,128]{1,0:T(8,128)S(1)} %bitcast.206, ...), kind=kLoop, calls=%fused_computation.16 | loop fusion | flops 7077888 | bytes 8919040 | tf_op jit(solution)/shard_map/convert_element_type | solution.py:86
  69.7 1.7 copy.126
  71.4 1.4 copy-done.22
  75.1 1.3 copy.237
  76.4 1.5 copy.130
  78.0 1.4 copy.134
  83.1 4.2 %constant_dynamic-update-slice_fusion.11 = (f32[8,512,128]{1,2,0:T(8,128)}, f32[7,512,128]{1,2,0:T(8,128)S(1)}) fusion(f32[8,512,128]{1,2,0:T(8,128)} %copy.237, bf16[7,768,128]{2,1,0:T(8,128)(2,1)} %bitcast.197, bf16[512,768,1]{0,1,2:T(8,128)(2,1)S(1)} %bitcast.186, f32[8,128,512]{2,1,0:T(8,128)} %copy-done.4), kind=kOutput, calls=%fused_computation.95 | convolution fusion | flops 705101824 | bytes 7667712 | tf_op jit(solution)/shard_map/sp,tpk->tsk/dot_general | solution.py:90
  87.3 2.0 constant_dynamic-update-slice_fusion.10
  89.3 1.8 constant_dynamic-update-slice_fusion.9
  91.1 1.6 constant_dynamic-update-slice_fusion.8
  92.7 1.4 constant_dynamic-update-slice_fusion.7
  95.2 2.2 fusion.32
  97.5 1.9 copy.154
  99.4 1.6 copy.155
  101.0 6.1 %all-to-all-start = ((f32[64,8,8,128]{3,2,1,0:T(8,128)}), f32[64,8,8,128]{3,2,1,0:T(8,128)S(1)}, u32[]{:S(2)}, u32[]{:S(2)}) async-start(f32[64,8,8,128]{3,2,1,0:T(8,128)} %copy.155), calls=%async_computation | async-start | bytes 4194304 | tf_op jit(solution)/shard_map/all_to_all | solution.py:31
  107.1 50.0 %all-to-all-done = f32[64,8,8,128]{3,2,1,0:T(8,128)S(1)} async-done(((f32[64,8,8,128]{3,2,1,0:T(8,128)}), f32[64,8,8,128]{3,2,1,0:T(8,128)S(1)}, u32[]{:S(2)}, u32[]{:S(2)}) %all-to-all-start) | async-done | bytes 2097184 | tf_op jit(solution)/shard_map/all_to_all | solution.py:31
  157.9 3.5 %all-to-all-start.1 = ((f32[4,8,8,128]{3,2,1,0:T(8,128)}), f32[4,8,8,128]{3,2,1,0:T(8,128)S(1)}, u32[]{:S(2)}, u32[]{:S(2)}) async-start(f32[4,8,8,128]{3,2,1,0:T(8,128)} %broadcast_in_dim.4), calls=%async_computation.1 | async-start | bytes 262144 | tf_op jit(solution)/shard_map/all_to_all | solution.py:37
  161.4 4.5 %all-to-all-done.1 = f32[4,8,8,128]{3,2,1,0:T(8,128)S(1)} async-done(((f32[4,8,8,128]{3,2,1,0:T(8,128)}), f32[4,8,8,128]{3,2,1,0:T(8,128)S(1)}, u32[]{:S(2)}, u32[]{:S(2)}) %all-to-all-start.1) | async-done | bytes 131104 | tf_op jit(solution)/shard_map/all_to_all | solution.py:37
  167.2 7.5 %all-to-all-start.2 = ((bf16[64,8,8,128]{3,2,1,0:T(8,128)(2,1)}), bf16[64,8,8,128]{3,2,1,0:T(8,128)(2,1)S(1)}, u32[]{:S(2)}, u32[]{:S(2)}) async-start(bf16[64,8,8,128]{3,2,1,0:T(8,128)(2,1)} %broadcast_in_dim.5), calls=%async_computation.2 | async-start | bytes 2097152 | tf_op jit(solution)/shard_map/all_to_all | solution.py:37
  176.0 28.0 %all-to-all-done.2 = bf16[64,8,8,128]{3,2,1,0:T(8,128)(2,1)S(1)} async-done(((bf16[64,8,8,128]{3,2,1,0:T(8,128)(2,1)}), bf16[64,8,8,128]{3,2,1,0:T(8,128)(2,1)S(1)}, u32[]{:S(2)}, u32[]{:S(2)}) %all-to-all-start.2) | async-done | bytes 1048608 | tf_op jit(solution)/shard_map/all_to_all | solution.py:37
  212.6 2.4 copy.172
  215.0 2.4 copy.173
  217.7 3.8 %collective-permute-start.4 = (f32[8,1,1,128,128]{3,4,2,1,0:T(8,128)S(1)}, f32[8,1,1,128,128]{3,4,2,1,0:T(8,128)S(1)}, u32[]{:S(2)}, u32[]{:S(2)}) collective-permute-start(f32[8,1,1,128,128]{3,4,2,1,0:T(8,128)S(1)} %get-tuple-element.227), channel_id=1, source_target_pairs={{1,0},{2,1},{3,2},{4,3},{5,4},{6,5},{7,6},{8,7},{9,8},{10,9},{11,1... | collective-permute-start | bytes 1572872 | tf_op jit(solution)/shard_map/ppermute | solution.py:17
  221.5 2.0 collective-permute-start.5
  223.6 7.8 %collective-permute-done.4 = f32[8,1,1,128,128]{3,4,2,1,0:T(8,128)S(1)} collective-permute-done((f32[8,1,1,128,128]{3,4,2,1,0:T(8,128)S(1)}, f32[8,1,1,128,128]{3,4,2,1,0:T(8,128)S(1)}, u32[]{:S(2)}, u32[]{:S(2)}) %collective-permute-start.4) | collective-permute-done | bytes 524320 | tf_op jit(solution)/shard_map/ppermute | solution.py:17
  231.4 8.7 %collective-permute-done.5 = f32[8,1,1,128,128]{3,4,2,1,0:T(8,128)S(1)} collective-permute-done((f32[8,1,1,128,128]{3,4,2,1,0:T(8,128)S(1)}, f32[8,1,1,128,128]{3,4,2,1,0:T(8,128)S(1)}, u32[]{:S(2)}, u32[]{:S(2)}) %collective-permute-start.5) | collective-permute-done | bytes 524320 | tf_op jit(solution)/shard_map/ppermute | solution.py:15
  240.1 1.8 broadcast_multiply_fusion
  242.0 1.9 collective-permute-start.6
  243.9 3.9 %collective-permute-start.7 = (f32[8,1,1,128,128]{3,4,2,1,0:T(8,128)S(1)}, f32[8,1,1,128,128]{3,4,2,1,0:T(8,128)S(1)}, u32[]{:S(2)}, u32[]{:S(2)}) collective-permute-start(f32[8,1,1,128,128]{3,4,2,1,0:T(8,128)S(1)} %get-tuple-element.226), channel_id=1, source_target_pairs={{0,1},{1,2},{2,3},{3,4},{4,5},{5,6},{6,7},{7,8},{8,9},{9,10},{10,1... | collective-permute-start | bytes 1572872 | tf_op jit(solution)/shard_map/ppermute | solution.py:15
  247.9 6.1 %collective-permute-done.6 = f32[8,1,1,128,128]{3,4,2,1,0:T(8,128)S(1)} collective-permute-done((f32[8,1,1,128,128]{3,4,2,1,0:T(8,128)S(1)}, f32[8,1,1,128,128]{3,4,2,1,0:T(8,128)S(1)}, u32[]{:S(2)}, u32[]{:S(2)}) %collective-permute-start.6) | collective-permute-done | bytes 524320 | tf_op jit(solution)/shard_map/ppermute | solution.py:17
  253.9 7.7 %collective-permute-done.7 = f32[8,1,1,128,128]{3,4,2,1,0:T(8,128)S(1)} collective-permute-done((f32[8,1,1,128,128]{3,4,2,1,0:T(8,128)S(1)}, f32[8,1,1,128,128]{3,4,2,1,0:T(8,128)S(1)}, u32[]{:S(2)}, u32[]{:S(2)}) %collective-permute-start.7) | collective-permute-done | bytes 524320 | tf_op jit(solution)/shard_map/ppermute | solution.py:15
  261.6 1.8 fusion.16
  263.4 2.4 copy.175
  (118 shorter events, 25.2 us)
Async XLA Ops:
  0.0 161.3 %copy-start = (f32[8,512]{1,0:T(8,128)S(1)}, f32[8,512]{1,0:T(8,128)}, u32[]{:S(2)}) copy-start(f32[8,512]{1,0:T(8,128)} %param.45) | copy-start | bytes 49156
  0.7 61.7 %copy-start.29 = (f32[1,6,128]{2,1,0:T(8,128)}, f32[1,6,128]{2,1,0:T(8,128)S(1)}, u32[]{:S(2)}) copy-start(f32[1,6,128]{2,1,0:T(8,128)S(1)} %copy.235) | copy-start | bytes 9220
  3.1 12.0 %copy-start.33 = (f32[1,6,128]{2,0,1:T(1,128)S(1)}, f32[1,6,128]{2,0,1:T(1,128)}, u32[]{:S(2)}) copy-start(f32[1,6,128]{2,0,1:T(1,128)} %param.42) | copy-start | bytes 9220
  3.5 20.9 %collective-permute-start = (f32[8,1,1,128,128]{3,4,2,1,0:T(8,128)S(1)}, f32[8,1,1,128,128]{3,4,2,1,0:T(8,128)S(1)}, u32[]{:S(2)}, u32[]{:S(2)}) collective-permute-start(f32[8,1,1,128,128]{3,4,2,1,0:T(8,128)S(1)} %get-tuple-element.231), channel_id=1, source_target_pairs={{1,0},{2,1},{3,2},{4,3},{5,4},{6,5},{7,6},{8,7},{9,8},{10,9},{11,1... | collective-permute-start | bytes 1572872 | tf_op jit(solution)/shard_map/ppermute | solution.py:17
  13.2 21.0 %collective-permute-start.1 = (f32[8,1,1,128,128]{3,4,2,1,0:T(8,128)S(1)}, f32[8,1,1,128,128]{3,4,2,1,0:T(8,128)S(1)}, u32[]{:S(2)}, u32[]{:S(2)}) collective-permute-start(f32[8,1,1,128,128]{3,4,2,1,0:T(8,128)S(1)} %get-tuple-element.232), channel_id=1, source_target_pairs={{0,1},{1,2},{2,3},{3,4},{4,5},{5,6},{6,7},{7,8},{8,9},{9,10},{10,1... | collective-permute-start | bytes 1572872 | tf_op jit(solution)/shard_map/ppermute | solution.py:15
  15.1 47.2 %copy-start.31 = (f32[1,6,128]{2,1,0:T(8,128)}, f32[1,6,128]{2,1,0:T(8,128)S(1)}, u32[]{:S(2)}) copy-start(f32[1,6,128]{2,1,0:T(8,128)S(1)} %copy.236) | copy-start | bytes 9220
  34.2 11.6 %slice-start.6 = ((s8[6291456]{0:T(1024)(128)(4,1)}), s8[4194304]{0:T(1024)(128)(4,1)S(1)}, s32[]{:S(2)}) async-start(s8[6291456]{0:T(1024)(128)(4,1)} %bitcast.180), calls=%async_computation.9 | async-start | bytes 8388608
  34.2 11.6 %slice-start.7 = ((s8[6291456]{0:T(1024)(128)(4,1)}), s8[2097152]{0:T(1024)(128)(4,1)S(1)}, s32[]{:S(2)}) async-start(s8[6291456]{0:T(1024)(128)(4,1)} %bitcast.180), calls=%async_computation.10 | async-start | bytes 4194304
  37.2 1.7 copy-start.5
  40.0 20.0 %collective-permute-start.2 = (f32[8,1,1,128,128]{3,4,2,1,0:T(8,128)}, f32[8,1,1,128,128]{3,4,2,1,0:T(8,128)}, u32[]{:S(2)}, u32[]{:S(2)}) collective-permute-start(f32[8,1,1,128,128]{3,4,2,1,0:T(8,128)} %get-tuple-element.229), channel_id=1, source_target_pairs={{1,0},{2,1},{3,2},{4,3},{5,4},{6,5},{7,6},{8,7},{9,8},{10,9},{11,1... | collective-permute-start | bytes 1572872 | tf_op jit(solution)/shard_map/ppermute | solution.py:17
  41.9 20.5 %collective-permute-start.3 = (f32[8,1,1,128,128]{3,4,2,1,0:T(8,128)}, f32[8,1,1,128,128]{3,4,2,1,0:T(8,128)}, u32[]{:S(2)}, u32[]{:S(2)}) collective-permute-start(f32[8,1,1,128,128]{3,4,2,1,0:T(8,128)} %get-tuple-element.230), channel_id=1, source_target_pairs={{0,1},{1,2},{2,3},{3,4},{4,5},{5,6},{6,7},{7,8},{8,9},{9,10},{10,1... | collective-permute-start | bytes 1572872 | tf_op jit(solution)/shard_map/ppermute | solution.py:15
  49.3 22.1 %copy-start.18 = (bf16[1,512,1,6,128]{1,4,3,2,0:T(8,128)(2,1)}, bf16[1,512,1,6,128]{1,4,3,2,0:T(8,128)(2,1)S(1)}, u32[]{:S(2)}) copy-start(bf16[1,512,1,6,128]{1,4,3,2,0:T(8,128)(2,1)S(1)} %copy.220) | copy-start | bytes 2359300
  69.7 1.7 copy-start.2
  71.4 1.4 copy-start.22
  73.8 1.3 copy-start.4
  73.8 2.6 slice-start
  75.1 2.8 %slice-start.1 = ((bf16[8,1,6,128,128]{3,4,2,1,0:T(8,128)(2,1)}), bf16[6,1,6,128,128]{3,4,2,1,0:T(8,128)(2,1)S(1)}, s32[]{:S(2)}) async-start(bf16[8,1,6,128,128]{3,4,2,1,0:T(8,128)(2,1)} %copy-done.2), calls=%async_computation.4 | async-start | bytes 2359296 | tf_op jit(solution)/shard_map/slice | solution.py:93
  76.4 3.0 %slice-start.2 = ((bf16[8,1,6,128,128]{3,4,2,1,0:T(8,128)(2,1)}), bf16[5,1,6,128,128]{3,4,2,1,0:T(8,128)(2,1)S(1)}, s32[]{:S(2)}) async-start(bf16[8,1,6,128,128]{3,4,2,1,0:T(8,128)(2,1)} %copy-done.2), calls=%async_computation.5 | async-start | bytes 1966080 | tf_op jit(solution)/shard_map/slice | solution.py:93
  78.0 2.8 %slice-start.3 = ((bf16[8,1,6,128,128]{3,4,2,1,0:T(8,128)(2,1)}), bf16[4,1,6,128,128]{3,4,2,1,0:T(8,128)(2,1)S(1)}, s32[]{:S(2)}) async-start(bf16[8,1,6,128,128]{3,4,2,1,0:T(8,128)(2,1)} %copy-done.2), calls=%async_computation.6 | async-start | bytes 1572864 | tf_op jit(solution)/shard_map/slice | solution.py:93
  78.0 3.1 %slice-start.4 = ((bf16[8,1,6,128,128]{3,4,2,1,0:T(8,128)(2,1)}), bf16[3,1,6,128,128]{3,4,2,1,0:T(8,128)(2,1)S(1)}, s32[]{:S(2)}) async-start(bf16[8,1,6,128,128]{3,4,2,1,0:T(8,128)(2,1)} %copy-done.2), calls=%async_computation.7 | async-start | bytes 1179648 | tf_op jit(solution)/shard_map/slice | solution.py:93
  79.4 2.8 %slice-start.5 = ((bf16[8,1,6,128,128]{3,4,2,1,0:T(8,128)(2,1)}), bf16[2,1,6,128,128]{3,4,2,1,0:T(8,128)(2,1)S(1)}, s32[]{:S(2)}) async-start(bf16[8,1,6,128,128]{3,4,2,1,0:T(8,128)(2,1)} %copy-done.2), calls=%async_computation.8 | async-start | bytes 786432 | tf_op jit(solution)/shard_map/slice | solution.py:93
  79.4 3.7 %copy-start.12 = (bf16[1,512,1,6,128]{1,4,3,2,0:T(8,128)(2,1)S(1)}, bf16[1,512,1,6,128]{1,4,3,2,0:T(8,128)(2,1)}, u32[]{:S(2)}) copy-start(bf16[1,512,1,6,128]{1,4,3,2,0:T(8,128)(2,1)} %copy.221) | copy-start | bytes 2359300
  83.1 4.2 %copy-start.10 = (bf16[1,512,1,6,128]{1,4,3,2,0:T(8,128)(2,1)S(1)}, bf16[1,512,1,6,128]{1,4,3,2,0:T(8,128)(2,1)}, u32[]{:S(2)}) copy-start(bf16[1,512,1,6,128]{1,4,3,2,0:T(8,128)(2,1)} %copy.222) | copy-start | bytes 2359300
  83.1 4.2 %copy-start.23 = (bf16[6,1,6,128,128]{4,3,2,0,1:T(8,128)(2,1)S(1)}, bf16[6,1,6,128,128]{4,3,2,0,1:T(8,128)(2,1)}, u32[]{:S(2)}) copy-start(bf16[6,1,6,128,128]{4,3,2,0,1:T(8,128)(2,1)} %copy.134) | copy-start | bytes 3538948
  87.3 2.0 copy-start.16
  87.3 2.0 copy-start.24
  89.3 1.8 copy-start.14
  91.1 1.6 copy-start.8
  91.1 1.6 copy-start.27
  91.1 3.0 %copy-start.20 = (bf16[1,512,1,6,128]{1,4,3,2,0:T(8,128)(2,1)S(1)}, bf16[1,512,1,6,128]{1,4,3,2,0:T(8,128)(2,1)}, u32[]{:S(2)}) copy-start(bf16[1,512,1,6,128]{1,4,3,2,0:T(8,128)(2,1)} %copy.226) | copy-start | bytes 2359300
  91.1 3.0 %copy-start.28 = (bf16[2,1,6,128,128]{4,3,2,0,1:T(8,128)(2,1)S(1)}, bf16[2,1,6,128,128]{4,3,2,0,1:T(8,128)(2,1)}, u32[]{:S(2)}) copy-start(bf16[2,1,6,128,128]{4,3,2,0,1:T(8,128)(2,1)} %copy.150) | copy-start | bytes 1179652
  92.7 2.6 copy-start.3
  101.0 56.1 %all-to-all-start = ((f32[64,8,8,128]{3,2,1,0:T(8,128)}), f32[64,8,8,128]{3,2,1,0:T(8,128)S(1)}, u32[]{:S(2)}, u32[]{:S(2)}) async-start(f32[64,8,8,128]{3,2,1,0:T(8,128)} %copy.155), calls=%async_computation | async-start | bytes 4194304 | tf_op jit(solution)/shard_map/all_to_all | solution.py:31
  107.1 67.7 %copy-start.25 = (bf16[1,512,1,6,128]{4,1,3,2,0:T(8,128)(2,1)S(1)}, bf16[1,512,1,6,128]{4,1,3,2,0:T(8,128)(2,1)}, u32[]{:S(2)}) copy-start(bf16[1,512,1,6,128]{4,1,3,2,0:T(8,128)(2,1)} %get-tuple-element.217) | copy-start | bytes 2359300
  157.2 46.9 %copy-start.19 = (bf16[1,512,1,6,128]{1,4,3,2,0:T(8,128)(2,1)S(1)}, bf16[1,512,1,6,128]{1,4,3,2,0:T(8,128)(2,1)}, u32[]{:S(2)}) copy-start(bf16[1,512,1,6,128]{1,4,3,2,0:T(8,128)(2,1)} %copy-done.18) | copy-start | bytes 2359300
  157.9 8.1 %all-to-all-start.1 = ((f32[4,8,8,128]{3,2,1,0:T(8,128)}), f32[4,8,8,128]{3,2,1,0:T(8,128)S(1)}, u32[]{:S(2)}, u32[]{:S(2)}) async-start(f32[4,8,8,128]{3,2,1,0:T(8,128)} %broadcast_in_dim.4), calls=%async_computation.1 | async-start | bytes 262144 | tf_op jit(solution)/shard_map/all_to_all | solution.py:37
  167.2 36.8 %all-to-all-start.2 = ((bf16[64,8,8,128]{3,2,1,0:T(8,128)(2,1)}), bf16[64,8,8,128]{3,2,1,0:T(8,128)(2,1)S(1)}, u32[]{:S(2)}, u32[]{:S(2)}) async-start(bf16[64,8,8,128]{3,2,1,0:T(8,128)(2,1)} %broadcast_in_dim.5), calls=%async_computation.2 | async-start | bytes 2097152 | tf_op jit(solution)/shard_map/all_to_all | solution.py:37
  205.1 1.2 copy-start.7
  205.1 1.4 copy-start.13
  209.5 1.2 copy-start.9
  210.7 1.4 copy-start.26
  215.0 2.4 copy-start.30
  217.4 22.7 %copy-start.32 = (f32[1,6,128]{2,1,0:T(8,128)S(1)}, f32[1,6,128]{2,1,0:T(8,128)}, u32[]{:S(2)}) copy-start(f32[1,6,128]{2,1,0:T(8,128)} %copy-done.31) | copy-start | bytes 9220
  217.7 13.7 %collective-permute-start.4 = (f32[8,1,1,128,128]{3,4,2,1,0:T(8,128)S(1)}, f32[8,1,1,128,128]{3,4,2,1,0:T(8,128)S(1)}, u32[]{:S(2)}, u32[]{:S(2)}) collective-permute-start(f32[8,1,1,128,128]{3,4,2,1,0:T(8,128)S(1)} %get-tuple-element.227), channel_id=1, source_target_pairs={{1,0},{2,1},{3,2},{4,3},{5,4},{6,5},{7,6},{8,7},{9,8},{10,9},{11,1... | collective-permute-start | bytes 1572872 | tf_op jit(solution)/shard_map/ppermute | solution.py:17
  221.5 18.5 %collective-permute-start.5 = (f32[8,1,1,128,128]{3,4,2,1,0:T(8,128)S(1)}, f32[8,1,1,128,128]{3,4,2,1,0:T(8,128)S(1)}, u32[]{:S(2)}, u32[]{:S(2)}) collective-permute-start(f32[8,1,1,128,128]{3,4,2,1,0:T(8,128)S(1)} %get-tuple-element.228), channel_id=1, source_target_pairs={{0,1},{1,2},{2,3},{3,4},{4,5},{5,6},{6,7},{7,8},{8,9},{9,10},{10,1... | collective-permute-start | bytes 1572872 | tf_op jit(solution)/shard_map/ppermute | solution.py:15
  242.0 11.9 %collective-permute-start.6 = (f32[8,1,1,128,128]{3,4,2,1,0:T(8,128)S(1)}, f32[8,1,1,128,128]{3,4,2,1,0:T(8,128)S(1)}, u32[]{:S(2)}, u32[]{:S(2)}) collective-permute-start(f32[8,1,1,128,128]{3,4,2,1,0:T(8,128)S(1)} %get-tuple-element.225), channel_id=1, source_target_pairs={{1,0},{2,1},{3,2},{4,3},{5,4},{6,5},{7,6},{8,7},{9,8},{10,9},{11,1... | collective-permute-start | bytes 1572872 | tf_op jit(solution)/shard_map/ppermute | solution.py:17
  243.9 17.7 %collective-permute-start.7 = (f32[8,1,1,128,128]{3,4,2,1,0:T(8,128)S(1)}, f32[8,1,1,128,128]{3,4,2,1,0:T(8,128)S(1)}, u32[]{:S(2)}, u32[]{:S(2)}) collective-permute-start(f32[8,1,1,128,128]{3,4,2,1,0:T(8,128)S(1)} %get-tuple-element.226), channel_id=1, source_target_pairs={{0,1},{1,2},{2,3},{3,4},{4,5},{5,6},{6,7},{7,8},{8,9},{9,10},{10,1... | collective-permute-start | bytes 1572872 | tf_op jit(solution)/shard_map/ppermute | solution.py:15
  261.6 4.2 %copy-start.1 = (f32[8,512]{1,0:T(8,128)S(1)}, f32[8,512]{1,0:T(8,128)}, u32[]{:S(2)}) copy-start(f32[8,512]{1,0:T(8,128)} %param.45) | copy-start | bytes 49156
  (5 other events, 5.6 us)
where the time goes:
time: 267 us; the launch traced here: 266 us
  waiting for transfers between devices  134 us (50%)
  local copies, waits for them, and re-layouts  49.5 us (19%)
  starting transfers between devices  46.2 us (17%)
  matrix products  20.8 us (8%)
  other arithmetic  14.7 us (6%)
    all_to_all x1, waiting for transfers between devices, sum_at_owner(): pieces = lax.all_to_all(cut_along(x, dim, length), axis, 0, 0, tiled=True)  50 us
    all_to_all x2, waiting for transfers between devices, from_everyone(): return lax.all_to_all(copies, axis, split_axis=0, concat_axis=0, tiled=True)  32.6 us
    ppermute x4, waiting for transfers between devices, with_halo(): lax.ppermute(tail, axis, [(i, (i + 1) % count) for i in range(ends)])  28.5 us
    unnamed x84, local copies, waits for them, and re-layouts  23.8 us
    ppermute x4, waiting for transfers between devices, with_halo(): lax.ppermute(head, axis, [((i + 1) % count, i) for i in range(ends)])  23.1 us
    ppermute x4, starting transfers between devices, with_halo(): lax.ppermute(head, axis, [((i + 1) % count, i) for i in range(ends)])  17.4 us
    dot_general x8, matrix products, body(): jnp.einsum('sp,tpk->tsk', kern_flat[lag], smoothed[:steps - lag], preferr...  15.3 us
    ppermute x4, starting transfers between devices, with_halo(): lax.ppermute(tail, axis, [(i, (i + 1) % count) for i in range(ends)])  11.8 us
  transfers between devices with their start and end apart: 11, of which 10 were waited for; matrix products, arithmetic and copies ran while one was open for 6% of the time, Pallas kernels for 0%

commit v1 on v0

v1 whole, which is shorter than its diff:
```python
import functools

import jax
import jax.numpy as jnp
from jax import lax
from jax.experimental import pallas as pl
from jax.experimental.pallas import tpu as pltpu
from jax.sharding import PartitionSpec as P

F32 = jnp.float32
BF16 = jnp.bfloat16
MESH = pl.DeviceIdType.MESH
COLS = 128
PAD = 8


def beside(ref, row):
    return ref[row, pl.ds(PAD - 1, COLS), :] + ref[row, pl.ds(PAD + 1, COLS), :]


def clear_pads(ref, rows):
    zero = jnp.zeros((PAD, ref.shape[2]), F32)
    for row in range(rows):
        ref[row, 0:PAD, :] = zero
        ref[row, PAD + COLS : 2 * PAD + COLS, :] = zero


def two_sweeps(rows, value, cpl, dia, coupled, again, swept, put):
    body = pl.ds(PAD, COLS)
    for j in range(rows + 4):
        coupled[j, body, :] = cpl[j] * value(j)
    for j in range(1, rows + 3):
        near = coupled[j - 1, body, :] + coupled[j + 1, body, :] + beside(coupled, j)
        once = dia[j - 1] * value(j) - cpl[j] * near
        swept[j - 1] = once
        again[j - 1, body, :] = cpl[j] * once
    for r in range(rows):
        q = r + 1
        near = again[q - 1, body, :] + again[q + 1, body, :] + beside(again, q)
        put(r, dia[q] * swept[q] - cpl[q + 1] * near)


class Place:
    def __init__(self, sizes):
        self.nyl, self.nyh, self.nx, self.nz = sizes
        self.tiles = self.nyh * self.nx * self.nz
        self.band = lax.axis_index("band")
        self.tile = lax.axis_index("tile")
        self.core = lax.rem(self.band, 2)
        self.z = lax.rem(self.tile, self.nz)
        self.plane = self.nyl * self.nyh * self.nx
        self.g = self.band // 2 * (self.nyh * self.nx) + self.tile // self.nz

    def twin(self):
        return (self.band + 1 - 2 * self.core, self.tile)

    def in_plane(self, d):
        g = lax.rem(self.g + d, self.plane)
        inner = self.nyh * self.nx
        return g, (g // inner * 2 + self.core, lax.rem(g, inner) * self.nz + self.z)

    def along_z(self, d):
        z = lax.rem(self.z + d, self.nz)
        return (self.band, self.tile - self.z + z)

    def row_neighbour(self, step):
        return (self.band, lax.rem(self.tile + step + self.tiles, self.tiles))


def remote(src, dst, send, recv, where):
    return pltpu.make_async_remote_copy(
        src_ref=src, dst_ref=dst, send_sem=send, recv_sem=recv, device_id=where, device_id_type=MESH
    )


def main_kernel(
    sizes,
    sketch_hbm, diag_ref, couple_ref, kern_hbm, prec_ref,
    adj_hbm, edge_hbm, coef_hbm,
    kv, kt, sk, stage, hin, smooth, total, pair_in, xsend, xin, zsend, zin, wsend, wgt, adj, edge_out,
    coef_in, cpl, dia, coupled, again, swept,
    load_sem, coef_send, coef_recv, halo_send, halo_recv, pair_send, pair_recv, x_send, x_recv,
    z_send, z_recv, g_send, g_recv, p_send, p_recv, edge_send, edge_recv, out_sem,
):
    here = Place(sizes)
    steps, rows, sensors, _ = kv.shape
    points = rows * COLS
    chunks = steps // 2
    half = sensors // 2
    piece = half // here.plane
    others = here.plane - 1
    zothers = here.nz - 1
    up, down = here.row_neighbour(-1), here.row_neighbour(1)
    has_up, has_down = here.tile > 0, here.tile < here.tiles - 1
    twin = here.twin()

    sketch_loads = [
        pltpu.make_async_copy(sketch_hbm.at[t, 0], sk.at[t], load_sem.at[t]) for t in range(steps)
    ]
    kern_loads = [
        pltpu.make_async_copy(kern_hbm.at[lag, 0], kv.at[lag], load_sem.at[steps + lag])
        for lag in range(steps)
    ]
    for load in sketch_loads:
        load.start()
    for load in kern_loads:
        load.start()

    barrier = pltpu.get_barrier_semaphore()
    greeted = [up, down, twin]
    greeted += [here.in_plane(d)[1] for d in range(1, here.plane)]
    greeted += [here.along_z(d) for d in range(1, here.nz)]
    for where in greeted:
        pl.semaphore_signal(barrier, inc=1, device_id=where, device_id_type=MESH)

    clear_pads(coupled, rows + 4)
    clear_pads(again, rows + 2)
    smooth[0] = jnp.zeros((points, COLS), BF16)
    wgt[steps] = jnp.zeros((sensors, COLS), BF16)
    adj[...] = jnp.zeros(adj.shape, F32)

    @pl.when(jnp.logical_not(has_up))
    def _():
        hin[:, 0] = jnp.zeros((steps, 2 * COLS, COLS), BF16)

    @pl.when(jnp.logical_not(has_down))
    def _():
        hin[:, 1] = jnp.zeros((steps, 2 * COLS, COLS), BF16)

    for t in range(2):
        sketch_loads[t].wait()
        stage[t, 0] = sk[t, 0:2].reshape(2 * COLS, COLS).astype(BF16)
        stage[t, 1] = sk[t, rows - 2 : rows].reshape(2 * COLS, COLS).astype(BF16)

    pl.semaphore_wait(barrier, len(greeted))

    def coef_copies(side, where):
        return [
            remote(ref, coef_in.at[side, i], coef_send.at[side, i], coef_recv.at[side, i], where)
            for i, ref in enumerate((couple_ref, diag_ref))
        ]

    def halo_copy(t, side, where):
        return remote(
            stage.at[t, 1 - side], hin.at[t, side], halo_send.at[t, side], halo_recv.at[t, side], where
        )

    def edge_copy(t, side, where):
        return remote(
            edge_out.at[t, 1 - side], edge_hbm.at[t, side], edge_send.at[t, side], edge_recv.at[t, side], where
        )

    def send_halos(t, copy):
        @pl.when(has_up)
        def _():
            copy(t, 1, up).start()

        @pl.when(has_down)
        def _():
            copy(t, 0, down).start()

    def wait_halos(t, copy):
        @pl.when(has_up)
        def _():
            copy(t, 0, up).wait_recv()
            copy(t, 1, up).wait_send()

        @pl.when(has_down)
        def _():
            copy(t, 1, down).wait_recv()
            copy(t, 0, down).wait_send()

    @pl.when(has_up)
    def _():
        for copy in coef_copies(1, up):
            copy.start()

    @pl.when(has_down)
    def _():
        for copy in coef_copies(0, down):
            copy.start()

    for t in range(steps):
        if t >= 2:
            sketch_loads[t].wait()
            stage[t, 0] = sk[t, 0:2].reshape(2 * COLS, COLS).astype(BF16)
            stage[t, 1] = sk[t, rows - 2 : rows].reshape(2 * COLS, COLS).astype(BF16)
        send_halos(t, halo_copy)

    def over_lanes(row):
        return jnp.broadcast_to(row, (COLS, COLS)).T

    for r in range(rows):
        cpl[r + 2] = over_lanes(couple_ref[r])
        dia[r + 1] = over_lanes(diag_ref[r])

    blank = jnp.zeros((COLS, COLS), F32)

    @pl.when(has_up)
    def _():
        for copy in coef_copies(0, up):
            copy.wait_recv()
        for copy in coef_copies(1, up):
            copy.wait_send()
        cpl[0] = over_lanes(coef_in[0, 0, rows - 2])
        cpl[1] = over_lanes(coef_in[0, 0, rows - 1])
        dia[0] = over_lanes(coef_in[0, 1, rows - 1])

    @pl.when(jnp.logical_not(has_up))
    def _():
        cpl[0] = blank
        cpl[1] = blank
        dia[0] = blank

    @pl.when(has_down)
    def _():
        for copy in coef_copies(1, down):
            copy.wait_recv()
        for copy in coef_copies(0, down):
            copy.wait_send()
        cpl[rows + 2] = over_lanes(coef_in[1, 0, 0])
        cpl[rows + 3] = over_lanes(coef_in[1, 0, 1])
        dia[rows + 1] = over_lanes(coef_in[1, 1, 0])

    @pl.when(jnp.logical_not(has_down))
    def _():
        cpl[rows + 2] = blank
        cpl[rows + 3] = blank
        dia[rows + 1] = blank

    coef_out = [
        pltpu.make_async_copy(cpl, coef_hbm.at[0 : rows + 4], out_sem.at[steps]),
        pltpu.make_async_copy(dia, coef_hbm.at[rows + 4 : 2 * rows + 6], out_sem.at[steps + 1]),
    ]
    for copy in coef_out:
        copy.start()

    my_half = pl.multiple_of(here.core * half, half)
    twin_half = pl.multiple_of(half - here.core * half, half)
    my_piece = pl.multiple_of(here.g * piece, piece)
    my_sensors = pl.multiple_of(here.core * half + here.g * piece, piece)

    def smooth_step(t):
        wait_halos(t, halo_copy)

        def value(j):
            if j < 2:
                return hin[t, 0, j * COLS : (j + 1) * COLS, :].astype(F32)
            if j < rows + 2:
                return sk[t, j - 2]
            j = j - rows - 2
            return hin[t, 1, j * COLS : (j + 1) * COLS, :].astype(F32)

        def put(r, field):
            smooth[t + 1, r * COLS : (r + 1) * COLS, :] = field.astype(BF16)

        two_sweeps(rows, value, cpl, dia, coupled, again, swept, put)

    def pair_copy(c):
        return remote(
            total.at[c, pl.ds(twin_half, half)], pair_in.at[c], pair_send.at[c], pair_recv.at[c], twin
        )

    def forward(c):
        for t in (2 * c, 2 * c + 1):
            kern_loads[t].wait()

        def per_step(t, carry):
            smooth_step(t)
            return carry

        lax.fori_loop(2 * c, 2 * c + 2, per_step, 0)
        total[c] = jnp.zeros((sensors, 2 * COLS), F32)

        def per_lag(lag, carry):
            lhs = jnp.concatenate([kv[lag, r] for r in range(rows)], axis=1)
            rhs = jnp.concatenate([smooth[2 * c - lag + 1], smooth[2 * c - lag + 2]], axis=1)
            total[c] += jnp.dot(lhs, rhs, preferred_element_type=F32)
            return carry

        lax.fori_loop(0, 2 * c + 2, per_lag, 0)
        pair_copy(c).start()

    def plane_copies(c):
        copies = []
        for d in range(1, here.plane):
            g, where = here.in_plane(d)
            copies.append(
                remote(
                    xsend.at[c, pl.ds(pl.multiple_of(g * piece, piece), piece)],
                    xin.at[c, pl.ds((d - 1) * piece, piece)],
                    x_send.at[c], x_recv.at[c], where,
                )
            )
        return copies

    def bulk(c, send, recv):
        block = xin.at[c]
        return remote(block, block, send, recv, twin)

    def to_plane(c):
        pair_copy(c).wait()
        xsend[c] = (total[c, pl.ds(my_half, half)] + pair_in[c]).astype(BF16)
        for copy in plane_copies(c):
            copy.start()

    def z_copies(c):
        return [
            remote(zsend.at[c], zin.at[c, d - 1], z_send.at[c, d], z_recv.at[c, d], here.along_z(d))
            for d in range(1, here.nz)
        ]

    def own_sum(c):
        rows_here = pl.ds(pl.multiple_of(my_half + my_piece, piece), piece)
        acc = total[c, rows_here] + pair_in[c, pl.ds(my_piece, piece)]
        for d in range(others):
            acc = acc + xin[c, d * piece : (d + 1) * piece].astype(F32)
        return acc

    def to_z(c):
        bulk(c, x_send.at[c], x_recv.at[c]).wait()
        mine = own_sum(c)
        zin[c, zothers] = mine.astype(BF16)
        zsend[c] = mine.astype(BF16)
        for copy in z_copies(c):
            copy.start()

    def gather_copies(c):
        return [
            remote(
                wsend.at[c],
                wgt.at[pl.ds(2 * c, 2), pl.ds(my_sensors, piece)],
                g_send.at[c], g_recv.at[c], here.in_plane(d)[1],
            )
            for d in range(1, here.plane)
        ]

    spot = lax.broadcasted_iota(jnp.int32, (piece, sensors), 1)
    wanted = lax.broadcasted_iota(jnp.int32, (piece, sensors), 0) + my_sensors

    def to_gather(c):
        for copy in z_copies(c):
            copy.wait()
        acc = own_sum(c)
        for d in range(zothers):
            acc = acc + zin[c, d].astype(F32)
        for i in range(2):
            t = 2 * c + i
            scale = jnp.sum(
                jnp.where(spot == wanted, prec_ref[t : t + 1, :], 0.0), axis=1, keepdims=True
            )
            block = (acc[:, i * COLS : (i + 1) * COLS] * scale).astype(BF16)
            wsend[c, i] = block
            wgt[t, pl.ds(my_sensors, piece), :] = block
        for copy in gather_copies(c):
            copy.start()

    def twin_copy(c):
        block = wgt.at[pl.ds(2 * c, 2), pl.ds(my_half, half)]
        return remote(block, block, p_send.at[c], p_recv.at[c], twin)

    def to_twin(c):
        bulk(c, g_send.at[c], g_recv.at[c]).wait()
        twin_copy(c).start()

    def flip(lag, carry):
        for r in range(rows):
            kt[lag, r * COLS : (r + 1) * COLS, :] = kv[lag, r].T
        return carry

    def back(c, low, high):
        def per_lag(lag, carry):
            rhs = jnp.concatenate([wgt[2 * c + lag], wgt[2 * c + lag + 1]], axis=1)
            out = jnp.dot(kt[lag], rhs, preferred_element_type=F32)
            adj[2 * c] += out[:, :COLS]
            adj[2 * c + 1] += out[:, COLS:]
            return carry

        lax.fori_loop(low, high, per_lag, 0)

    def out_copy(t):
        return pltpu.make_async_copy(adj.at[t], adj_hbm.at[t], out_sem.at[t])

    def finish(c):
        for t in (2 * c, 2 * c + 1):
            edge_out[t, 0] = adj[t, 0 : 2 * COLS, :].astype(BF16)
            edge_out[t, 1] = adj[t, points - 2 * COLS : points, :].astype(BF16)
            send_halos(t, edge_copy)
            out_copy(t).start()

    last = chunks - 1
    for c in range(chunks):
        forward(c)
        if c >= 1:
            to_plane(c - 1)
        if c >= 2:
            to_z(c - 2)
        if c >= 3:
            to_gather(c - 3)
    to_plane(last)
    to_z(last - 1)
    to_gather(last - 2)
    to_twin(last - 3)
    lax.fori_loop(0, steps // 2, flip, 0)
    to_z(last)
    to_gather(last - 1)
    to_twin(last - 2)
    lax.fori_loop(steps // 2, steps, flip, 0)
    to_gather(last)
    to_twin(last - 1)
    for c in range(last):
        twin_copy(c).wait()
    early = steps - 2
    for c in range(last):
        back(c, 0, early - 2 * c - 1)
    to_twin(last)
    twin_copy(last).wait()
    for c in range(chunks):
        back(c, max(0, early - 2 * c - 1), steps - 2 * c)
        finish(c)
    for copy in coef_out:
        copy.wait()
    for t in range(steps):
        out_copy(t).wait()
        wait_halos(t, edge_copy)


def last_kernel(tiles, adj_ref, edge_ref, coef_ref, out_ref, coupled, again, swept):
    rows = out_ref.shape[2]
    tile = lax.axis_index("tile")

    @pl.when(pl.program_id(0) == 0)
    def _():
        clear_pads(coupled, rows + 4)
        clear_pads(again, rows + 2)

    def value(j):
        if j < 2:
            block = edge_ref[0, 0, j * COLS : (j + 1) * COLS, :].astype(F32)
            return jnp.where(tile > 0, block, 0.0)
        if j < rows + 2:
            return adj_ref[0, (j - 2) * COLS : (j - 1) * COLS, :]
        j = j - rows - 2
        block = edge_ref[0, 1, j * COLS : (j + 1) * COLS, :].astype(F32)
        return jnp.where(tile < tiles - 1, block, 0.0)

    def put(r, field):
        out_ref[0, 0, r] = field

    two_sweeps(
        rows, value, coef_ref.at[0 : rows + 4], coef_ref.at[rows + 4 : 2 * rows + 6], coupled, again, swept, put
    )


def split(mesh):
    bands, tiles = mesh.shape["band"], mesh.shape["tile"]
    if tiles == 64:
        return (bands // 2, 2, 4, 8)
    return (bands // 2, 1, tiles // 2, 2)


def body(sizes, sketch, diag_coef, couple, kernel, noise_prec):
    steps, _, rows, cols, width = sketch.shape
    sensors = kernel.shape[1]
    points = rows * cols
    nyl, nyh, nx, nz = sizes
    plane = nyl * nyh * nx
    tiles = nyh * nx * nz
    half = sensors // 2
    piece = half // plane
    chunks = steps // 2
    by_row = jnp.transpose(kernel, (0, 2, 3, 1, 4))
    diag_rows = jnp.transpose(diag_coef, (1, 0, 2))
    couple_rows = jnp.transpose(couple, (1, 0, 2))
    anywhere = pl.BlockSpec(memory_space=pl.ANY)
    near = pl.BlockSpec(memory_space=pltpu.VMEM)
    dma = pltpu.SemaphoreType.DMA
    sweep_scratch = [
        pltpu.VMEM((rows + 4, cols + 2 * PAD, width), F32),
        pltpu.VMEM((rows + 2, cols + 2 * PAD, width), F32),
        pltpu.VMEM((rows + 2, cols, width), F32),
    ]
    edge_shape = (steps, 2, 2 * cols, width)
    adj, edge, coef = pl.pallas_call(
        functools.partial(main_kernel, sizes),
        out_shape=(
            jax.ShapeDtypeStruct((steps, points, width), F32),
            jax.ShapeDtypeStruct(edge_shape, BF16),
            jax.ShapeDtypeStruct((2 * rows + 6, cols, width), F32),
        ),
        in_specs=[anywhere, near, near, anywhere, near],
        out_specs=(anywhere, anywhere, anywhere),
        scratch_shapes=[
            pltpu.VMEM((steps, rows, sensors, cols), BF16),
            pltpu.VMEM((steps, points, sensors), BF16),
            pltpu.VMEM((steps, rows, cols, width), F32),
            pltpu.VMEM(edge_shape, BF16),
            pltpu.VMEM(edge_shape, BF16),
            pltpu.VMEM((steps + 1, points, width), BF16),
            pltpu.VMEM((chunks, sensors, 2 * width), F32),
            pltpu.VMEM((chunks, half, 2 * width), F32),
            pltpu.VMEM((chunks, half, 2 * width), BF16),
            pltpu.VMEM((chunks, (plane - 1) * piece, 2 * width), BF16),
            pltpu.VMEM((chunks, piece, 2 * width), BF16),
            pltpu.VMEM((chunks, nz, piece, 2 * width), BF16),
            pltpu.VMEM((chunks, 2, piece, width), BF16),
            pltpu.VMEM((steps + 1, sensors, width), BF16),
            pltpu.VMEM((steps, points, width), F32),
            pltpu.VMEM(edge_shape, BF16),
            pltpu.VMEM((2, 2, rows, 1, cols), F32),
            pltpu.VMEM((rows + 4, cols, width), F32),
            pltpu.VMEM((rows + 2, cols, width), F32),
            *sweep_scratch,
            dma((2 * steps,)),
            dma((2, 2)), dma((2, 2)),
            dma((steps, 2)), dma((steps, 2)),
            dma((chunks,)), dma((chunks,)),
            dma((chunks,)), dma((chunks,)),
            dma((chunks, nz)), dma((chunks, nz)),
            dma((chunks,)), dma((chunks,)),
            dma((chunks,)), dma((chunks,)),
            dma((steps, 2)), dma((steps, 2)),
            dma((steps + 2,)),
        ],
        compiler_params=pltpu.CompilerParams(
            collective_id=0, has_side_effects=True, vmem_limit_bytes=56 * 1024 * 1024
        ),
        name="sketch_main",
    )(sketch, diag_rows, couple_rows, by_row, noise_prec)
    return pl.pallas_call(
        functools.partial(last_kernel, tiles),
        out_shape=jax.ShapeDtypeStruct(sketch.shape, F32),
        grid=(steps,),
        in_specs=[
            pl.BlockSpec((1, points, width), lambda t: (t, 0, 0)),
            pl.BlockSpec((1, 2, 2 * cols, width), lambda t: (t, 0, 0, 0)),
            pl.BlockSpec((2 * rows + 6, cols, width), lambda t: (0, 0, 0)),
        ],
        out_specs=pl.BlockSpec((1, 1, rows, cols, width), lambda t: (t, 0, 0, 0, 0)),
        scratch_shapes=sweep_scratch,
        compiler_params=pltpu.CompilerParams(vmem_limit_bytes=32 * 1024 * 1024),
        name="last_sweeps",
    )(adj, edge, coef)


def solution(mesh):
    placed = (
        P(None, "band", "tile", None, None),
        P("band", "tile", None),
        P("band", "tile", None),
        P(None, None, "band", "tile", None),
        P(),
    )
    return jax.shard_map(
        functools.partial(body, split(mesh)),
        mesh=mesh,
        in_specs=placed,
        out_specs=P(None, "band", "tile", None, None),
        check_vma=False,
    )
```

time: 267 us -> 79.3 us (0.30)
  waiting for transfers between devices: 134 us -> 0 us
  Pallas kernels: 0 us -> 74.3 us
  starting transfers between devices: 46.2 us -> 0 us
  local copies, waits for them, and re-layouts: 49.5 us -> 4.38 us
  matrix products: 20.8 us -> 0 us
  other arithmetic: 14.7 us -> 0 us
    all_to_all x3 -> x0, waiting for transfers between devices: 82.6 us -> none  [the longest x1 50 us: sum_at_owner(): pieces = lax.all_to_all(cut_along(x, dim, length), axis, 0, 0, tiled=True)]
    pallas_call x0 -> x2, Pallas kernels: none -> 74.3 us  [the longest x1 69.4 us: body(): pl.pallas_call(functools.partial(main_kernel, sizes), out_shape=(jax.Shap...]
    ppermute x8 -> x0, waiting for transfers between devices: 51.6 us -> none  [the longest x4 28.5 us: with_halo(): lax.ppermute(tail, axis, [(i, (i + 1) % count) for i in range(ends)])]
    ppermute x8 -> x0, starting transfers between devices: 29.2 us -> none  [the longest x4 17.4 us: with_halo(): lax.ppermute(head, axis, [((i + 1) % count, i) for i in range(ends)])]
    dot_general x16 -> x0, matrix products: 20.8 us -> none  [the longest x8 15.3 us: body(): jnp.einsum('sp,tpk->tsk', kern_flat[lag], smoothed[:steps - lag], preferr...]
    unnamed x84 -> x6, local copies, waits for them, and re-layouts: 23.8 us -> 4.38 us
    all_to_all x3 -> x0, starting transfers between devices: 17 us -> none  [the longest x2 11 us: from_everyone(): return lax.all_to_all(copies, axis, split_axis=0, concat_axis=0, tiled=True)]
    slice x24 -> x0, local copies, waits for them, and re-layouts: 11.2 us -> none  [the longest x18 6.66 us: body(): smoothed[:steps - lag]]
  transfers between devices with their start and end apart: 11 -> 0, of which waited for: 10 -> 0; matrix products, arithmetic and copies ran while one was open for 6% -> 0% of each run, Pallas kernels for 0% -> 0%
where the time goes in v1:
time: 79.3 us; the launch traced here: 78.7 us
  Pallas kernels  74.3 us (94%)
  local copies, waits for them, and re-layouts  4.38 us (6%)
    pallas_call x1, Pallas kernels, body(): pl.pallas_call(functools.partial(main_kernel, sizes), out_shape=(jax.Shap...  69.4 us
    pallas_call x1, Pallas kernels, body(): pl.pallas_call(functools.partial(last_kernel, tiles), out_shape=jax.Shape...  4.87 us
    unnamed x6, local copies, waits for them, and re-layouts  4.38 us

profile of v1, /device:TPU:16, one launch (start us, length us, event | category | flops | bytes accessed | tf_op | source)
XLA Modules:
  0.0 78.7 jit_solution(8851077592079551163)
XLA Ops:
  0.0 69.4 %sketch_main.1 = (f32[8,768,128]{2,1,0:T(8,128)}, bf16[8,2,256,128]{3,2,1,0:T(8,128)(2,1)}, f32[18,128,128]{2,1,0:T(8,128)}) custom-call(f32[8,1,6,128,128]{4,3,2,1,0:T(8,128)} %sketch_hbm.1, f32[6,1,128]{2,1,0:T(1,128)} %bitcast.4, f32[6,1,128]{2,1,0:T(1,128)} %bitcast.5, bf16[8,1,6,512,128]{4,3,2,1,0:T(8,128)(2,1)} %bitcast.3, f32[8,512]{1,0:T(8,128)} %prec_ref.1), custom_call_target="tpu_custom_call" | custom-call | tf_op jit(solution)/shard_map/sketch_main/pallas_call | solution.py:484
  69.4 0.0 copy-start
  69.4 1.9 %copy-done = f32[8,768,128]{2,1,0:T(8,128)S(1)} copy-done((f32[8,768,128]{2,1,0:T(8,128)S(1)}, f32[8,768,128]{2,1,0:T(8,128)}, u32[]{:S(2)}) %copy-start) | copy-done | bytes 3145752
  71.3 0.0 copy-start.1
  71.3 1.3 %copy-done.1 = f32[18,128,128]{2,1,0:T(8,128)S(1)} copy-done((f32[18,128,128]{2,1,0:T(8,128)S(1)}, f32[18,128,128]{2,1,0:T(8,128)}, u32[]{:S(2)}) %copy-start.1) | copy-done | bytes 1179672
  72.6 0.0 copy-start.2
  72.6 1.2 %copy-done.2 = bf16[8,2,256,128]{3,2,1,0:T(8,128)(2,1)S(1)} copy-done((bf16[8,2,256,128]{3,2,1,0:T(8,128)(2,1)S(1)}, bf16[8,2,256,128]{3,2,1,0:T(8,128)(2,1)}, u32[]{:S(2)}) %copy-start.2) | copy-done | bytes 1048600
  73.8 4.9 %last_sweeps.1 = f32[8,1,6,128,128]{4,3,2,1,0:T(8,128)} custom-call(f32[8,768,128]{2,1,0:T(8,128)S(1)} %copy-done, bf16[8,2,256,128]{3,2,1,0:T(8,128)(2,1)S(1)} %copy-done.2, f32[18,128,128]{2,1,0:T(8,128)S(1)} %copy-done.1), custom_call_target="tpu_custom_call" | custom-call | tf_op jit(solution)/shard_map/last_sweeps/pallas_call | solution.py:530
Async XLA Ops:
  69.4 1.9 %copy-start = (f32[8,768,128]{2,1,0:T(8,128)S(1)}, f32[8,768,128]{2,1,0:T(8,128)}, u32[]{:S(2)}) copy-start(f32[8,768,128]{2,1,0:T(8,128)} %get-tuple-element.8.adj_ref) | copy-start | bytes 9437188
  71.3 1.3 %copy-start.1 = (f32[18,128,128]{2,1,0:T(8,128)S(1)}, f32[18,128,128]{2,1,0:T(8,128)}, u32[]{:S(2)}) copy-start(f32[18,128,128]{2,1,0:T(8,128)} %get-tuple-element.10.coef_ref) | copy-start | bytes 3538948
  72.6 1.2 %copy-start.2 = (bf16[8,2,256,128]{3,2,1,0:T(8,128)(2,1)S(1)}, bf16[8,2,256,128]{3,2,1,0:T(8,128)(2,1)}, u32[]{:S(2)}) copy-start(bf16[8,2,256,128]{3,2,1,0:T(8,128)(2,1)} %get-tuple-element.9.edge_ref) | copy-start | bytes 3145732

commit v2 on v1

v2 whole, which is shorter than its diff:
```python
import functools

import jax
import jax.numpy as jnp
from jax import lax
from jax.experimental import pallas as pl
from jax.experimental.pallas import tpu as pltpu
from jax.sharding import PartitionSpec as P

F32 = jnp.float32
BF16 = jnp.bfloat16
MESH = pl.DeviceIdType.MESH
COLS = 128
PAD = 8


def beside(ref, row):
    return ref[row, pl.ds(PAD - 1, COLS), :] + ref[row, pl.ds(PAD + 1, COLS), :]


def clear_pads(ref, rows):
    zero = jnp.zeros((PAD, ref.shape[2]), F32)
    for row in range(rows):
        ref[row, 0:PAD, :] = zero
        ref[row, PAD + COLS : 2 * PAD + COLS, :] = zero


def two_sweeps(rows, value, cpl, dia, coupled, again, swept, put):
    body = pl.ds(PAD, COLS)
    for j in range(rows + 4):
        coupled[j, body, :] = cpl[j] * value(j)
    for j in range(1, rows + 3):
        near = coupled[j - 1, body, :] + coupled[j + 1, body, :] + beside(coupled, j)
        once = dia[j - 1] * value(j) - cpl[j] * near
        swept[j - 1] = once
        again[j - 1, body, :] = cpl[j] * once
    for r in range(rows):
        q = r + 1
        near = again[q - 1, body, :] + again[q + 1, body, :] + beside(again, q)
        put(r, dia[q] * swept[q] - cpl[q + 1] * near)


class Place:
    def __init__(self, sizes):
        self.nyl, self.nyh, self.nx, self.nz = sizes
        self.tiles = self.nyh * self.nx * self.nz
        self.band = lax.axis_index("band")
        self.tile = lax.axis_index("tile")
        self.core = lax.rem(self.band, 2)
        self.z = lax.rem(self.tile, self.nz)
        self.plane = self.nyl * self.nyh * self.nx
        self.g = self.band // 2 * (self.nyh * self.nx) + self.tile // self.nz

    def twin(self):
        return (self.band + 1 - 2 * self.core, self.tile)

    def in_plane(self, d):
        g = lax.rem(self.g + d, self.plane)
        inner = self.nyh * self.nx
        return g, (g // inner * 2 + self.core, lax.rem(g, inner) * self.nz + self.z)

    def along_z(self, d):
        z = lax.rem(self.z + d, self.nz)
        return (self.band, self.tile - self.z + z)

    def row_neighbour(self, step):
        return (self.band, lax.rem(self.tile + step + self.tiles, self.tiles))


def remote(src, dst, send, recv, where):
    return pltpu.make_async_remote_copy(
        src_ref=src, dst_ref=dst, send_sem=send, recv_sem=recv, device_id=where, device_id_type=MESH
    )


def main_kernel(
    sizes,
    sketch_hbm, diag_ref, couple_ref, kern_hbm, prec_ref,
    out_hbm,
    kv, kt, sk, field, stage, hin, smooth, total, pair_in, xsend, xin, zsend, zin, wsend, wgt, adj,
    edge_out, edge_in, coef_in, cpl, dia, coupled, again, swept,
    load_sem, coef_send, coef_recv, halo_send, halo_recv, pair_send, pair_recv, x_send, x_recv,
    z_send, z_recv, g_send, g_recv, p_send, p_recv, edge_send, edge_recv, out_sem,
):
    here = Place(sizes)
    steps, rows, sensors, _ = kv.shape
    points = rows * COLS
    chunks = steps // 2
    pairs = steps // 2
    half = sensors // 2
    piece = half // here.plane
    others = here.plane - 1
    zothers = here.nz - 1
    up, down = here.row_neighbour(-1), here.row_neighbour(1)
    has_up, has_down = here.tile > 0, here.tile < here.tiles - 1
    twin = here.twin()

    sketch_loads = [
        pltpu.make_async_copy(sketch_hbm.at[t, 0], sk.at[t], load_sem.at[t]) for t in range(steps)
    ]
    kern_loads = [
        pltpu.make_async_copy(kern_hbm.at[lag, 0], kv.at[lag], load_sem.at[steps + lag])
        for lag in range(steps)
    ]
    for load in sketch_loads:
        load.start()
    for load in kern_loads:
        load.start()

    barrier = pltpu.get_barrier_semaphore()
    greeted = [up, down, twin]
    greeted += [here.in_plane(d)[1] for d in range(1, here.plane)]
    greeted += [here.along_z(d) for d in range(1, here.nz)]
    for where in greeted:
        pl.semaphore_signal(barrier, inc=1, device_id=where, device_id_type=MESH)

    low = lax.broadcasted_iota(jnp.int32, (COLS, COLS), 1) < COLS // 2

    def turn(x):
        return pltpu.roll(x, COLS // 2, 1)

    clear_pads(coupled, rows + 4)
    clear_pads(again, rows + 2)
    for h in range(2):
        smooth[h, 0, 0] = jnp.zeros((points, COLS), BF16)
        smooth[h, 1, 0] = jnp.zeros((points, COLS), BF16)
        wgt[h, 0, pairs] = jnp.zeros((sensors, COLS), BF16)
        wgt[h, 1, pairs + 1] = jnp.zeros((sensors, COLS), BF16)

    @pl.when(jnp.logical_not(has_up))
    def _():
        hin[:, 0] = jnp.zeros((steps, 2 * COLS, COLS), BF16)
        edge_in[:, 0] = jnp.zeros((steps, 2 * COLS, COLS), BF16)

    @pl.when(jnp.logical_not(has_down))
    def _():
        hin[:, 1] = jnp.zeros((steps, 2 * COLS, COLS), BF16)
        edge_in[:, 1] = jnp.zeros((steps, 2 * COLS, COLS), BF16)

    for p in range(pairs):
        sketch_loads[2 * p].wait()
        sketch_loads[2 * p + 1].wait()

        def pack(r, carry, p=p):
            first, second = sk[2 * p, r], sk[2 * p + 1, r]
            field[p, r] = jnp.where(low, first, turn(second))
            field[pairs + p, r] = jnp.where(low, turn(first), second)
            return carry

        lax.fori_loop(0, rows, pack, 0)
        for f in (p, pairs + p):
            stage[f, 0] = field[f, 0:2].reshape(2 * COLS, COLS).astype(BF16)
            stage[f, 1] = field[f, rows - 2 : rows].reshape(2 * COLS, COLS).astype(BF16)

    pl.semaphore_wait(barrier, len(greeted))

    def coef_copies(side, where):
        return [
            remote(ref, coef_in.at[side, i], coef_send.at[side, i], coef_recv.at[side, i], where)
            for i, ref in enumerate((couple_ref, diag_ref))
        ]

    def halo_copy(f, side, where):
        return remote(
            stage.at[f, 1 - side], hin.at[f, side], halo_send.at[f, side], halo_recv.at[f, side], where
        )

    def edge_copy(f, side, where):
        return remote(
            edge_out.at[f, 1 - side], edge_in.at[f, side], edge_send.at[f, side], edge_recv.at[f, side], where
        )

    def send_halos(f, copy):
        @pl.when(has_up)
        def _():
            copy(f, 1, up).start()

        @pl.when(has_down)
        def _():
            copy(f, 0, down).start()

    def wait_halos(f, copy):
        @pl.when(has_up)
        def _():
            copy(f, 0, up).wait_recv()
            copy(f, 1, up).wait_send()

        @pl.when(has_down)
        def _():
            copy(f, 1, down).wait_recv()
            copy(f, 0, down).wait_send()

    @pl.when(has_up)
    def _():
        for copy in coef_copies(1, up):
            copy.start()

    @pl.when(has_down)
    def _():
        for copy in coef_copies(0, down):
            copy.start()

    for f in range(steps):
        send_halos(f, halo_copy)

    def over_lanes(row):
        return jnp.broadcast_to(row, (COLS, COLS)).T

    for r in range(rows):
        cpl[r + 2] = over_lanes(couple_ref[r])
        dia[r + 1] = over_lanes(diag_ref[r])

    blank = jnp.zeros((COLS, COLS), F32)

    @pl.when(jnp.logical_not(has_up))
    def _():
        cpl[0] = blank
        cpl[1] = blank
        dia[0] = blank

    @pl.when(jnp.logical_not(has_down))
    def _():
        cpl[rows + 2] = blank
        cpl[rows + 3] = blank
        dia[rows + 1] = blank

    def flip(lag, carry):
        for r in range(rows):
            kt[lag, r * COLS : (r + 1) * COLS, :] = kv[lag, r].T
        return carry

    for load in kern_loads:
        load.wait()
    lax.fori_loop(0, steps // 2, flip, 0)

    @pl.when(has_up)
    def _():
        for copy in coef_copies(0, up):
            copy.wait_recv()
        for copy in coef_copies(1, up):
            copy.wait_send()
        cpl[0] = over_lanes(coef_in[0, 0, rows - 2])
        cpl[1] = over_lanes(coef_in[0, 0, rows - 1])
        dia[0] = over_lanes(coef_in[0, 1, rows - 1])

    @pl.when(has_down)
    def _():
        for copy in coef_copies(1, down):
            copy.wait_recv()
        for copy in coef_copies(0, down):
            copy.wait_send()
        cpl[rows + 2] = over_lanes(coef_in[1, 0, 0])
        cpl[rows + 3] = over_lanes(coef_in[1, 0, 1])
        dia[rows + 1] = over_lanes(coef_in[1, 1, 0])

    my_half = pl.multiple_of(here.core * half, half)
    twin_half = pl.multiple_of(half - here.core * half, half)
    my_piece = pl.multiple_of(here.g * piece, piece)
    my_sensors = pl.multiple_of(here.core * half + here.g * piece, piece)

    def rows_of(own, edges, f):
        def value(j):
            if j < 2:
                return edges[f, 0, j * COLS : (j + 1) * COLS, :].astype(F32)
            if j < rows + 2:
                return own(j - 2)
            j = j - rows - 2
            return edges[f, 1, j * COLS : (j + 1) * COLS, :].astype(F32)

        return value

    def sweeps(value, put):
        two_sweeps(rows, value, cpl, dia, coupled, again, swept, put)

    def smooth_field(h, f):
        p = f - h * pairs
        wait_halos(f, halo_copy)

        def put(r, new):
            block = slice(r * COLS, (r + 1) * COLS)
            before = smooth[h, 0, p, block, :].astype(F32)
            smooth[h, 0, p + 1, block, :] = new.astype(BF16)
            smooth[h, 1, p + 1, block, :] = turn(jnp.where(low, new, before)).astype(BF16)

        sweeps(rows_of(lambda r: field[f, r], hin, f), put)

    def pair_copy(c):
        return remote(
            total.at[c, pl.ds(twin_half, half)], pair_in.at[c], pair_send.at[c], pair_recv.at[c], twin
        )

    def forward(c):
        h, q = c // 2, c % 2
        total[c] = jnp.zeros((sensors, 2 * COLS), F32)

        def per_lag(lag, carry):
            odd, at = lax.rem(lag, 2), 2 * q + 1 - lax.div(lag, 2)
            lhs = jnp.concatenate([kv[lag, r] for r in range(rows)], axis=1)
            rhs = jnp.concatenate([smooth[h, odd, at], smooth[h, odd, at + 1]], axis=1)
            total[c] += jnp.dot(lhs, rhs, preferred_element_type=F32)
            return carry

        if q:
            lax.fori_loop(4, 8, per_lag, 0)

        def per_field(f, carry):
            smooth_field(h, f)
            return carry

        lax.fori_loop(2 * c, 2 * c + 2, per_field, 0)
        lax.fori_loop(0, 4, per_lag, 0)
        pair_copy(c).start()

    def plane_copies(c):
        copies = []
        for d in range(1, here.plane):
            g, where = here.in_plane(d)
            copies.append(
                remote(
                    xsend.at[c, pl.ds(pl.multiple_of(g * piece, piece), piece)],
                    xin.at[c, pl.ds((d - 1) * piece, piece)],
                    x_send.at[c], x_recv.at[c], where,
                )
            )
        return copies

    def bulk(c, send, recv):
        block = xin.at[c]
        return remote(block, block, send, recv, twin)

    def to_plane(c):
        pair_copy(c).wait()
        xsend[c] = (total[c, pl.ds(my_half, half)] + pair_in[c]).astype(BF16)
        for copy in plane_copies(c):
            copy.start()

    def z_copies(c):
        return [
            remote(zsend.at[c], zin.at[c, d - 1], z_send.at[c, d], z_recv.at[c, d], here.along_z(d))
            for d in range(1, here.nz)
        ]

    def own_sum(c):
        rows_here = pl.ds(pl.multiple_of(my_half + my_piece, piece), piece)
        acc = total[c, rows_here] + pair_in[c, pl.ds(my_piece, piece)]
        for d in range(others):
            acc = acc + xin[c, d * piece : (d + 1) * piece].astype(F32)
        return acc

    def to_z(c):
        bulk(c, x_send.at[c], x_recv.at[c]).wait()
        zsend[c] = own_sum(c).astype(BF16)
        for copy in z_copies(c):
            copy.start()

    def gather_copies(c):
        h, q = c // 2, c % 2
        return [
            remote(
                wsend.at[c],
                wgt.at[h, 0, pl.ds(2 * q, 2), pl.ds(my_sensors, piece)],
                g_send.at[c], g_recv.at[c], here.in_plane(d)[1],
            )
            for d in range(1, here.plane)
        ]

    spot = lax.broadcasted_iota(jnp.int32, (piece, sensors), 1)
    wanted = lax.broadcasted_iota(jnp.int32, (piece, sensors), 0) + my_sensors
    left = lax.broadcasted_iota(jnp.int32, (piece, COLS), 1) < COLS // 2

    def scale_of(t):
        return jnp.sum(jnp.where(spot == wanted, prec_ref[t : t + 1, :], 0.0), axis=1, keepdims=True)

    def to_gather(c):
        h, q = c // 2, c % 2
        for copy in z_copies(c):
            copy.wait()
        acc = own_sum(c)
        for d in range(zothers):
            acc = acc + zin[c, d].astype(F32)
        for i in range(2):
            t = 4 * q + 2 * i
            scale = jnp.where(left, scale_of(t), scale_of(t + 1))
            block = (acc[:, i * COLS : (i + 1) * COLS] * scale).astype(BF16)
            wsend[c, i] = block
            wgt[h, 0, 2 * q + i, pl.ds(my_sensors, piece), :] = block
        for copy in gather_copies(c):
            copy.start()

    def twin_copy(c):
        h, q = c // 2, c % 2
        block = wgt.at[h, 0, pl.ds(2 * q, 2), pl.ds(my_half, half)]
        return remote(block, block, p_send.at[c], p_recv.at[c], twin)

    def to_twin(c):
        bulk(c, g_send.at[c], g_recv.at[c]).wait()
        twin_copy(c).start()

    def weights_in(c):
        h, q = c // 2, c % 2
        twin_copy(c).wait()
        for p in (2, 3, 4) if q else (1,):
            for s in range(0, sensors, COLS):
                block = slice(s, s + COLS)
                mixed = jnp.where(low, wgt[h, 0, p, block, :].astype(F32), wgt[h, 0, p - 1, block, :].astype(F32))
                wgt[h, 1, p, block, :] = turn(mixed).astype(BF16)

    def back(c):
        h, q = c // 2, c % 2
        adj[2 * c] = jnp.zeros((points, COLS), F32)
        adj[2 * c + 1] = jnp.zeros((points, COLS), F32)

        def per_lag(lag, carry):
            odd, at = lax.rem(lag, 2), 2 * q + lax.div(lag + 1, 2)
            rhs = jnp.concatenate([wgt[h, odd, at], wgt[h, odd, at + 1]], axis=1)
            out = jnp.dot(kt[lag], rhs, preferred_element_type=F32)
            adj[2 * c] += out[:, :COLS]
            adj[2 * c + 1] += out[:, COLS:]
            return carry

        lax.fori_loop(0, steps - 4 * q, per_lag, 0)
        for f in (2 * c, 2 * c + 1):
            edge_out[f, 0] = adj[f, 0 : 2 * COLS, :].astype(BF16)
            edge_out[f, 1] = adj[f, points - 2 * COLS : points, :].astype(BF16)
            send_halos(f, edge_copy)

    def out_copy(t):
        return pltpu.make_async_copy(sk.at[t], out_hbm.at[t, 0], out_sem.at[t])

    def result(f):
        wait_halos(f, edge_copy)
        return rows_of(lambda r: adj[f, pl.ds(r * COLS, COLS), :], edge_in, f)

    def first_half(p, carry):
        def put(r, new):
            field[p, r] = new

        sweeps(result(p), put)
        return carry

    def second_half(p, carry):
        def put(r, new):
            before = field[p, r]
            sk[2 * p, r] = jnp.where(low, before, turn(new))
            sk[2 * p + 1, r] = jnp.where(low, turn(before), new)

        sweeps(result(pairs + p), put)
        out_copy(2 * p).start()
        out_copy(2 * p + 1).start()
        return carry

    forward(0)
    forward(1)
    to_plane(0)
    forward(2)
    to_plane(1)
    to_z(0)
    forward(3)
    to_plane(2)
    to_z(1)
    to_plane(3)
    to_gather(0)
    lax.fori_loop(steps // 2, steps, flip, 0)
    to_z(2)
    to_gather(1)
    to_z(3)
    to_twin(0)
    to_gather(2)
    to_twin(1)
    to_gather(3)
    weights_in(0)
    weights_in(1)
    back(1)
    back(0)
    to_twin(2)
    to_twin(3)
    weights_in(2)
    weights_in(3)
    back(3)
    back(2)
    lax.fori_loop(2, 4, first_half, 0)
    lax.fori_loop(0, 2, first_half, 0)
    lax.fori_loop(2, 4, second_half, 0)
    lax.fori_loop(0, 2, second_half, 0)
    for t in range(steps):
        out_copy(t).wait()


def split(mesh):
    bands, tiles = mesh.shape["band"], mesh.shape["tile"]
    if tiles == 64:
        return (bands // 2, 2, 4, 8)
    return (bands // 2, 1, tiles // 2, 2)


def body(sizes, sketch, diag_coef, couple, kernel, noise_prec):
    steps, _, rows, cols, width = sketch.shape
    sensors = kernel.shape[1]
    points = rows * cols
    nyl, nyh, nx, nz = sizes
    plane = nyl * nyh * nx
    tiles = nyh * nx * nz
    half = sensors // 2
    piece = half // plane
    chunks = steps // 2
    by_row = jnp.transpose(kernel, (0, 2, 3, 1, 4))
    diag_rows = jnp.transpose(diag_coef, (1, 0, 2))
    couple_rows = jnp.transpose(couple, (1, 0, 2))
    anywhere = pl.BlockSpec(memory_space=pl.ANY)
    near = pl.BlockSpec(memory_space=pltpu.VMEM)
    dma = pltpu.SemaphoreType.DMA
    sweep_scratch = [
        pltpu.VMEM((rows + 4, cols + 2 * PAD, width), F32),
        pltpu.VMEM((rows + 2, cols + 2 * PAD, width), F32),
        pltpu.VMEM((rows + 2, cols, width), F32),
    ]
    edge_shape = (steps, 2, 2 * cols, width)
    return pl.pallas_call(
        functools.partial(main_kernel, sizes),
        out_shape=jax.ShapeDtypeStruct(sketch.shape, F32),
        in_specs=[anywhere, near, near, anywhere, near],
        out_specs=anywhere,
        scratch_shapes=[
            pltpu.VMEM((steps, rows, sensors, cols), BF16),
            pltpu.VMEM((steps, points, sensors), BF16),
            pltpu.VMEM((steps, rows, cols, width), F32),
            pltpu.VMEM((steps, rows, cols, width), F32),
            pltpu.VMEM(edge_shape, BF16),
            pltpu.VMEM(edge_shape, BF16),
            pltpu.VMEM((2, 2, chunks + 1, points, width), BF16),
            pltpu.VMEM((chunks, sensors, 2 * width), F32),
            pltpu.VMEM((chunks, half, 2 * width), F32),
            pltpu.VMEM((chunks, half, 2 * width), BF16),
            pltpu.VMEM((chunks, (plane - 1) * piece, 2 * width), BF16),
            pltpu.VMEM((chunks, piece, 2 * width), BF16),
            pltpu.VMEM((chunks, nz - 1, piece, 2 * width), BF16),
            pltpu.VMEM((chunks, 2, piece, width), BF16),
            pltpu.VMEM((2, 2, chunks + 2, sensors, width), BF16),
            pltpu.VMEM((steps, points, width), F32),
            pltpu.VMEM(edge_shape, BF16),
            pltpu.VMEM(edge_shape, BF16),
            pltpu.VMEM((2, 2, rows, 1, cols), F32),
            pltpu.VMEM((rows + 4, cols, width), F32),
            pltpu.VMEM((rows + 2, cols, width), F32),
            *sweep_scratch,
            dma((2 * steps,)),
            dma((2, 2)), dma((2, 2)),
            dma((steps, 2)), dma((steps, 2)),
            dma((chunks,)), dma((chunks,)),
            dma((chunks,)), dma((chunks,)),
            dma((chunks, nz)), dma((chunks, nz)),
            dma((chunks,)), dma((chunks,)),
            dma((chunks,)), dma((chunks,)),
            dma((steps, 2)), dma((steps, 2)),
            dma((steps,)),
        ],
        compiler_params=pltpu.CompilerParams(
            collective_id=0, has_side_effects=True, vmem_limit_bytes=60 * 1024 * 1024
        ),
        name="sketch_main",
    )(sketch, diag_rows, couple_rows, by_row, noise_prec)


def solution(mesh):
    placed = (
        P(None, "band", "tile", None, None),
        P("band", "tile", None),
        P("band", "tile", None),
        P(None, None, "band", "tile", None),
        P(),
    )
    return jax.shard_map(
        functools.partial(body, split(mesh)),
        mesh=mesh,
        in_specs=placed,
        out_specs=P(None, "band", "tile", None, None),
        check_vma=False,
    )
```

time: 79.3 us -> 68.9 us (0.87)
  Pallas kernels: 74.3 us -> 64.4 us
    pallas_call x2 -> x1, Pallas kernels: 74.3 us -> 64.4 us  [body(): pl.pallas_call(functools.partial(main_kernel, sizes), out_shape=jax.Shape...]
    unnamed x6 -> x1, local copies, waits for them, and re-layouts: 4.38 us -> 3.91 us
where the time goes in v2:
time: 68.9 us; the launch traced here: 68.3 us
  Pallas kernels  64.4 us (93%)
  local copies, waits for them, and re-layouts  3.91 us (6%)
    pallas_call x1, Pallas kernels, body(): pl.pallas_call(functools.partial(main_kernel, sizes), out_shape=jax.Shape...  64.4 us
    unnamed x1, local copies, waits for them, and re-layouts  3.91 us

profile of v2, /device:TPU:16, one launch (start us, length us, event | category | flops | bytes accessed | tf_op | source)
XLA Modules:
  0.0 68.3 jit_solution(110247199209696516)
XLA Ops:
  0.0 64.4 %sketch_main.1 = f32[8,1,6,128,128]{4,3,2,1,0:T(8,128)} custom-call(f32[8,1,6,128,128]{4,3,2,1,0:T(8,128)} %sketch_hbm.1, f32[6,1,128]{2,1,0:T(1,128)} %bitcast.4, f32[6,1,128]{2,1,0:T(1,128)} %bitcast.5, bf16[8,1,6,512,128]{4,3,2,1,0:T(8,128)(2,1)} %bitcast.3, f32[8,512]{1,0:T(8,128)} %prec_ref.1), custom_call_target="tpu_custom_call" | custom-call | tf_op jit(solution)/shard_map/sketch_main/pallas_call | solution.py:518
  64.4 3.9 %copy.7 = f32[8,1,6,128,128]{4,3,2,1,0:T(8,128)} copy(f32[8,1,6,128,128]{4,3,2,1,0:T(8,128)} %sketch_main.1) | data formatting | bytes 6291456

commit v3 on v2

--- a/solution.py
+++ b/solution.py
@@ -75,8 +75,9 @@
 
 def main_kernel(
     sizes,
-    sketch_hbm, diag_ref, couple_ref, kern_hbm, prec_ref,
+    sketch_hbm, diag_hbm, couple_hbm, kern_hbm, prec_hbm,
     out_hbm,
+    diag_ref, couple_ref, prec_ref,
     kv, kt, sk, field, stage, hin, smooth, total, pair_in, xsend, xin, zsend, zin, wsend, wgt, adj,
     edge_out, edge_in, coef_in, cpl, dia, coupled, again, swept,
     load_sem, coef_send, coef_recv, halo_send, halo_recv, pair_send, pair_recv, x_send, x_recv,
@@ -102,25 +103,97 @@
         pltpu.make_async_copy(kern_hbm.at[lag, 0], kv.at[lag], load_sem.at[steps + lag])
         for lag in range(steps)
     ]
-    for load in sketch_loads:
-        load.start()
-    for load in kern_loads:
-        load.start()
-
+    small_loads = [
+        pltpu.make_async_copy(src, dst, load_sem.at[2 * steps + i])
+        for i, (src, dst) in enumerate(
+            ((couple_hbm, couple_ref), (diag_hbm, diag_ref), (prec_hbm, prec_ref))
+        )
+    ]
     barrier = pltpu.get_barrier_semaphore()
     greeted = [up, down, twin]
     greeted += [here.in_plane(d)[1] for d in range(1, here.plane)]
     greeted += [here.along_z(d) for d in range(1, here.nz)]
+    for load in sketch_loads:
+        load.start()
     for where in greeted:
         pl.semaphore_signal(barrier, inc=1, device_id=where, device_id_type=MESH)
+    for load in small_loads + kern_loads:
+        load.start()
 
     low = lax.broadcasted_iota(jnp.int32, (COLS, COLS), 1) < COLS // 2
 
     def turn(x):
         return pltpu.roll(x, COLS // 2, 1)
 
+    def coef_copies(side, where):
+        return [
+            remote(ref, coef_in.at[side, i], coef_send.at[side, i], coef_recv.at[side, i], where)
+            for i, ref in enumerate((couple_hbm, diag_hbm))
+        ]
+
+    def halo_copy(f, side, where):
+        return remote(
+            stage.at[f, 1 - side], hin.at[f, side], halo_send.at[f, side], halo_recv.at[f, side], where
+        )
+
+    def edge_copy(f, side, where):
+        return remote(
+            edge_out.at[f, 1 - side], edge_in.at[f, side], edge_send.at[f, side], edge_recv.at[f, side], where
+        )
+
+    def send_halos(f, copy):
+        @pl.when(has_up)
+        def _():
+            copy(f, 1, up).start()
+
+        @pl.when(has_down)
+        def _():
+            copy(f, 0, down).start()
+
+    def wait_halos(f, copy):
+        @pl.when(has_up)
+        def _():
+            copy(f, 0, up).wait_recv()
+            copy(f, 1, up).wait_send()
+
+        @pl.when(has_down)
+        def _():
+            copy(f, 1, down).wait_recv()
+            copy(f, 0, down).wait_send()
+
+    for p in range(pairs):
+        sketch_loads[2 * p].wait()
+        sketch_loads[2 * p + 1].wait()
+
+        for r in range(rows):
+            first, second = sk[2 * p, r], sk[2 * p + 1, r]
+            crossed = turn(jnp.where(low, second, first))
+            field[p, r] = jnp.where(low, first, crossed)
+            field[pairs + p, r] = jnp.where(low, crossed, second)
+        for f in (p, pairs + p):
+            stage[f, 0] = field[f, 0:2].reshape(2 * COLS, COLS).astype(BF16)
+            stage[f, 1] = field[f, rows - 2 : rows].reshape(2 * COLS, COLS).astype(BF16)
+        if p == 0:
+            pl.semaphore_wait(barrier, len(greeted))
+
+            @pl.when(has_up)
+            def _():
+                for copy in coef_copies(1, up):
+                    copy.start()
+
+            @pl.when(has_down)
+            def _():
+                for copy in coef_copies(0, down):
+                    copy.start()
+
+        send_halos(p, halo_copy)
+    for p in range(pairs):
+        send_halos(pairs + p, halo_copy)
+
     clear_pads(coupled, rows + 4)
     clear_pads(again, rows + 2)
+    total[...] = jnp.zeros(total.shape, F32)
+    adj[...] = jnp.zeros(adj.shape, F32)
     for h in range(2):
         smooth[h, 0, 0] = jnp.zeros((points, COLS), BF16)
         smooth[h, 1, 0] = jnp.zeros((points, COLS), BF16)
@@ -137,71 +210,8 @@
         hin[:, 1] = jnp.zeros((steps, 2 * COLS, COLS), BF16)
         edge_in[:, 1] = jnp.zeros((steps, 2 * COLS, COLS), BF16)
 
-    for p in range(pairs):
-        sketch_loads[2 * p].wait()
-        sketch_loads[2 * p + 1].wait()
-
-        def pack(r, carry, p=p):
-            first, second = sk[2 * p, r], sk[2 * p + 1, r]
-            field[p, r] = jnp.where(low, first, turn(second))
-            field[pairs + p, r] = jnp.where(low, turn(first), second)
-            return carry
-
-        lax.fori_loop(0, rows, pack, 0)
-        for f in (p, pairs + p):
-            stage[f, 0] = field[f, 0:2].reshape(2 * COLS, COLS).astype(BF16)
-            stage[f, 1] = field[f, rows - 2 : rows].reshape(2 * COLS, COLS).astype(BF16)
-
-    pl.semaphore_wait(barrier, len(greeted))
-
-    def coef_copies(side, where):
-        return [
-            remote(ref, coef_in.at[side, i], coef_send.at[side, i], coef_recv.at[side, i], where)
-            for i, ref in enumerate((couple_ref, diag_ref))
-        ]
-
-    def halo_copy(f, side, where):
-        return remote(
-            stage.at[f, 1 - side], hin.at[f, side], halo_send.at[f, side], halo_recv.at[f, side], where
-        )
-
-    def edge_copy(f, side, where):
-        return remote(
-            edge_out.at[f, 1 - side], edge_in.at[f, side], edge_send.at[f, side], edge_recv.at[f, side], where
-        )
-
-    def send_halos(f, copy):
-        @pl.when(has_up)
-        def _():
-            copy(f, 1, up).start()
-
-        @pl.when(has_down)
-        def _():
-            copy(f, 0, down).start()
-
-    def wait_halos(f, copy):
-        @pl.when(has_up)
-        def _():
-            copy(f, 0, up).wait_recv()
-            copy(f, 1, up).wait_send()
-
-        @pl.when(has_down)
-        def _():
-            copy(f, 1, down).wait_recv()
-            copy(f, 0, down).wait_send()
-
-    @pl.when(has_up)
-    def _():
-        for copy in coef_copies(1, up):
-            copy.start()
-
-    @pl.when(has_down)
-    def _():
-        for copy in coef_copies(0, down):
-            copy.start()
-
-    for f in range(steps):
-        send_halos(f, halo_copy)
+    for load in small_loads:
+        load.wait()
 
     def over_lanes(row):
         return jnp.broadcast_to(row, (COLS, COLS)).T
@@ -229,8 +239,8 @@
             kt[lag, r * COLS : (r + 1) * COLS, :] = kv[lag, r].T
         return carry
 
-    for load in kern_loads:
-        load.wait()
+    for lag in range(steps // 2):
+        kern_loads[lag].wait()
     lax.fori_loop(0, steps // 2, flip, 0)
 
     @pl.when(has_up)
@@ -289,27 +299,54 @@
             total.at[c, pl.ds(twin_half, half)], pair_in.at[c], pair_send.at[c], pair_recv.at[c], twin
         )
 
-    def forward(c):
-        h, q = c // 2, c % 2
-        total[c] = jnp.zeros((sensors, 2 * COLS), F32)
-
-        def per_lag(lag, carry):
-            odd, at = lax.rem(lag, 2), 2 * q + 1 - lax.div(lag, 2)
-            lhs = jnp.concatenate([kv[lag, r] for r in range(rows)], axis=1)
-            rhs = jnp.concatenate([smooth[h, odd, at], smooth[h, odd, at + 1]], axis=1)
-            total[c] += jnp.dot(lhs, rhs, preferred_element_type=F32)
-            return carry
-
-        if q:
-            lax.fori_loop(4, 8, per_lag, 0)
-
-        def per_field(f, carry):
-            smooth_field(h, f)
-            return carry
-
-        lax.fori_loop(2 * c, 2 * c + 2, per_field, 0)
-        lax.fori_loop(0, 4, per_lag, 0)
-        pair_copy(c).start()
+    def lags_dot(lags, lhs, rhs):
+        left_side = jnp.concatenate([x for lag in lags for x in lhs(lag)], axis=1)
+        right_side = jnp.concatenate([jnp.concatenate(rhs(lag), axis=1) for lag in lags], axis=0)
+        return jnp.dot(left_side, right_side, preferred_element_type=F32)
+
+    def at_step(step, wanted, *actions):
+        @pl.when(step == wanted)
+        def _():
+            for action in actions:
+                action()
+
+    def forward(k, carry):
+        h, i = k // 3, lax.rem(k, 3)
+        q = (i + 1) // 2
+        c = 2 * h + q
+        fresh = i != 1
+        start = jnp.where(fresh, 0, 4)
+
+        at_step(k, 1, rest_of_kernel)
+        at_step(k, 2, lambda: to_plane(0))
+        at_step(k, 5, lambda: to_z(0), lambda: to_plane(2))
+
+        @pl.when(fresh)
+        def _():
+            def per_field(f, inner):
+                smooth_field(h, f)
+                return inner
+
+            lax.fori_loop(2 * c, 2 * c + 2, per_field, 0)
+
+        at_step(k, 3, lambda: to_plane(1))
+        at_step(k, 5, lambda: to_z(1))
+        first = 2 * q + 1 - start // 2
+
+        def lhs(lag):
+            return [kv[start + lag, r] for r in range(rows)]
+
+        def rhs(lag):
+            odd, at = lag % 2, first - lag // 2
+            return [smooth[h, odd, at], smooth[h, odd, at + 1]]
+
+        total[c] += lags_dot(range(4), lhs, rhs)
+
+        @pl.when(fresh)
+        def _():
+            pair_copy(c).start()
+
+        return carry
 
     def plane_copies(c):
         copies = []
@@ -405,24 +442,33 @@
                 mixed = jnp.where(low, wgt[h, 0, p, block, :].astype(F32), wgt[h, 0, p - 1, block, :].astype(F32))
                 wgt[h, 1, p, block, :] = turn(mixed).astype(BF16)
 
-    def back(c):
-        h, q = c // 2, c % 2
-        adj[2 * c] = jnp.zeros((points, COLS), F32)
-        adj[2 * c + 1] = jnp.zeros((points, COLS), F32)
-
-        def per_lag(lag, carry):
-            odd, at = lax.rem(lag, 2), 2 * q + lax.div(lag + 1, 2)
-            rhs = jnp.concatenate([wgt[h, odd, at], wgt[h, odd, at + 1]], axis=1)
-            out = jnp.dot(kt[lag], rhs, preferred_element_type=F32)
-            adj[2 * c] += out[:, :COLS]
-            adj[2 * c + 1] += out[:, COLS:]
-            return carry
-
-        lax.fori_loop(0, steps - 4 * q, per_lag, 0)
-        for f in (2 * c, 2 * c + 1):
-            edge_out[f, 0] = adj[f, 0 : 2 * COLS, :].astype(BF16)
-            edge_out[f, 1] = adj[f, points - 2 * COLS : points, :].astype(BF16)
-            send_halos(f, edge_copy)
+    def back(k, carry):
+        h, i = k // 3, lax.rem(k, 3)
+        q = jnp.where(i == 0, 1, 0)
+        c = 2 * h + q
+        start = jnp.where(i == 2, 4, 0)
+        at_step(k, 3, lambda: to_twin(2), lambda: to_twin(3), lambda: weights_in(2), lambda: weights_in(3))
+        first = 2 * q + start // 2
+
+        def lhs(lag):
+            return [kt[start + lag]]
+
+        def rhs(lag):
+            odd, at = lag % 2, first + (lag + 1) // 2
+            return [wgt[h, odd, at], wgt[h, odd, at + 1]]
+
+        out = lags_dot(range(4), lhs, rhs)
+        adj[2 * c] += out[:, :COLS]
+        adj[2 * c + 1] += out[:, COLS:]
+
+        @pl.when(i != 1)
+        def _():
+            for f in (2 * c, 2 * c + 1):
+                edge_out[f, 0] = adj[f, 0 : 2 * COLS, :].astype(BF16)
+                edge_out[f, 1] = adj[f, points - 2 * COLS : points, :].astype(BF16)
+                send_halos(f, edge_copy)
+
+        return carry
 
     def out_copy(t):
         return pltpu.make_async_copy(sk.at[t], out_hbm.at[t, 0], out_sem.at[t])
@@ -431,36 +477,37 @@
         wait_halos(f, edge_copy)
         return rows_of(lambda r: adj[f, pl.ds(r * COLS, COLS), :], edge_in, f)
 
-    def first_half(p, carry):
+    def first_half(k, carry):
+        p = lax.rem(k + 2, pairs)
+
         def put(r, new):
             field[p, r] = new
 
         sweeps(result(p), put)
         return carry
 
-    def second_half(p, carry):
+    def second_half(k, carry):
+        p = lax.rem(k + 2, pairs)
+
         def put(r, new):
             before = field[p, r]
-            sk[2 * p, r] = jnp.where(low, before, turn(new))
-            sk[2 * p + 1, r] = jnp.where(low, turn(before), new)
+            crossed = turn(jnp.where(low, new, before))
+            sk[2 * p, r] = jnp.where(low, before, crossed)
+            sk[2 * p + 1, r] = jnp.where(low, crossed, new)
 
         sweeps(result(pairs + p), put)
         out_copy(2 * p).start()
         out_copy(2 * p + 1).start()
         return carry
 
-    forward(0)
-    forward(1)
-    to_plane(0)
-    forward(2)
-    to_plane(1)
-    to_z(0)
-    forward(3)
-    to_plane(2)
-    to_z(1)
+    def rest_of_kernel():
+        for lag in range(steps // 2, steps):
+            kern_loads[lag].wait()
+
+    lax.fori_loop(0, 6, forward, 0)
     to_plane(3)
+    lax.fori_loop(steps // 2, steps, flip, 0)
     to_gather(0)
-    lax.fori_loop(steps // 2, steps, flip, 0)
     to_z(2)
     to_gather(1)
     to_z(3)
@@ -470,18 +517,9 @@
     to_gather(3)
     weights_in(0)
     weights_in(1)
-    back(1)
-    back(0)
-    to_twin(2)
-    to_twin(3)
-    weights_in(2)
-    weights_in(3)
-    back(3)
-    back(2)
-    lax.fori_loop(2, 4, first_half, 0)
-    lax.fori_loop(0, 2, first_half, 0)
-    lax.fori_loop(2, 4, second_half, 0)
-    lax.fori_loop(0, 2, second_half, 0)
+    lax.fori_loop(0, 6, back, 0)
+    lax.fori_loop(0, pairs, first_half, 0)
+    lax.fori_loop(0, pairs, second_half, 0)
     for t in range(steps):
         out_copy(t).wait()
 
@@ -507,7 +545,10 @@
     diag_rows = jnp.transpose(diag_coef, (1, 0, 2))
     couple_rows = jnp.transpose(couple, (1, 0, 2))
     anywhere = pl.BlockSpec(memory_space=pl.ANY)
-    near = pl.BlockSpec(memory_space=pltpu.VMEM)
+
+    def far(x):
+        return pltpu.with_memory_space_constraint(x, pltpu.HBM)
+
     dma = pltpu.SemaphoreType.DMA
     sweep_scratch = [
         pltpu.VMEM((rows + 4, cols + 2 * PAD, width), F32),
@@ -518,9 +559,12 @@
     return pl.pallas_call(
         functools.partial(main_kernel, sizes),
         out_shape=jax.ShapeDtypeStruct(sketch.shape, F32),
-        in_specs=[anywhere, near, near, anywhere, near],
+        in_specs=[pl.BlockSpec(memory_space=pltpu.HBM)] * 5,
         out_specs=anywhere,
         scratch_shapes=[
+            pltpu.VMEM(diag_rows.shape, F32),
+            pltpu.VMEM(couple_rows.shape, F32),
+            pltpu.VMEM(noise_prec.shape, F32),
             pltpu.VMEM((steps, rows, sensors, cols), BF16),
             pltpu.VMEM((steps, points, sensors), BF16),
             pltpu.VMEM((steps, rows, cols, width), F32),
@@ -543,7 +587,7 @@
             pltpu.VMEM((rows + 4, cols, width), F32),
             pltpu.VMEM((rows + 2, cols, width), F32),
             *sweep_scratch,
-            dma((2 * steps,)),
+            dma((2 * steps + 3,)),
             dma((2, 2)), dma((2, 2)),
             dma((steps, 2)), dma((steps, 2)),
             dma((chunks,)), dma((chunks,)),
@@ -555,10 +599,10 @@
             dma((steps,)),
         ],
         compiler_params=pltpu.CompilerParams(
-            collective_id=0, has_side_effects=True, vmem_limit_bytes=60 * 1024 * 1024
+            collective_id=0, has_side_effects=True, vmem_limit_bytes=48 * 1024 * 1024
         ),
         name="sketch_main",
-    )(sketch, diag_rows, couple_rows, by_row, noise_prec)
+    )(sketch, far(diag_rows), far(couple_rows), by_row, far(noise_prec))
 
 
 def solution(mesh):

time: 68.9 us -> 62.1 us (0.901)
  Pallas kernels: 64.4 us -> 60 us
  local copies, waits for them, and re-layouts: 3.91 us -> 1.67 us
    pallas_call x1, Pallas kernels: 64.4 us -> 60 us  [body(): pl.pallas_call(functools.partial(main_kernel, sizes), out_shape=jax.Shape...]
    unnamed x1, local copies, waits for them, and re-layouts: 3.91 us -> 1.67 us
where the time goes in v3:
time: 62.1 us; the launch traced here: 61.7 us
  Pallas kernels  60 us (97%)
  local copies, waits for them, and re-layouts  1.67 us (3%)
    pallas_call x1, Pallas kernels, body(): pl.pallas_call(functools.partial(main_kernel, sizes), out_shape=jax.Shape...  60 us
    unnamed x1, local copies, waits for them, and re-layouts  1.67 us

profile of v3, /device:TPU:16, one launch (start us, length us, event | category | flops | bytes accessed | tf_op | source)
XLA Modules:
  0.0 61.7 jit_solution(15760400018820771790)
XLA Ops:
  0.0 60.0 %sketch_main.1 = f32[8,1,6,128,128]{4,3,2,1,0:T(8,128)S(1)} custom-call(f32[8,1,6,128,128]{4,3,2,1,0:T(8,128)} %sketch_hbm.1, f32[6,1,128]{2,1,0:T(1,128)} %bitcast.4, f32[6,1,128]{2,1,0:T(1,128)} %bitcast.5, bf16[8,1,6,512,128]{4,3,2,1,0:T(8,128)(2,1)} %bitcast.3, f32[8,512]{1,0:T(8,128)} %prec_hbm.1), custom_call_target="tpu_custom_call" | custom-call | tf_op jit(solution)/shard_map/sketch_main/pallas_call | solution.py:559
  60.0 1.7 %copy.7 = f32[8,1,6,128,128]{4,3,2,1,0:T(8,128)} copy(f32[8,1,6,128,128]{4,3,2,1,0:T(8,128)S(1)} %sketch_main.1) | data formatting | bytes 6291456

commit v4 on v3

--- a/solution.py
+++ b/solution.py
@@ -55,9 +55,23 @@
         return (self.band + 1 - 2 * self.core, self.tile)
 
     def in_plane(self, d):
-        g = lax.rem(self.g + d, self.plane)
+        sizes = (self.nyl, self.nyh, self.nx)
         inner = self.nyh * self.nx
-        return g, (g // inner * 2 + self.core, lax.rem(g, inner) * self.nz + self.z)
+        steps = (d // inner, d % inner // self.nx, d % self.nx)
+        own = (self.g // inner, lax.rem(self.g, inner) // self.nx, lax.rem(self.g, self.nx))
+        yl, yh, x = (lax.rem(o + step, n) for o, step, n in zip(own, steps, sizes))
+        return yl * inner + yh * self.nx + x, (yl * 2 + self.core, (yh * self.nx + x) * self.nz + self.z)
+
+    def plane_offsets(self):
+        def hops(d):
+            x = d % self.nx
+            yl, yh = d // (self.nyh * self.nx), d // self.nx % self.nyh
+            return min(x, self.nx - x) + (1 if yl else 2 * yh)
+
+        return sorted(range(1, self.plane), key=hops, reverse=True)
+
+    def z_offsets(self):
+        return sorted(range(1, self.nz), key=lambda d: min(d, self.nz - d), reverse=True)
 
     def along_z(self, d):
         z = lax.rem(self.z + d, self.nz)
@@ -97,14 +111,15 @@
     twin = here.twin()
 
     sketch_loads = [
-        pltpu.make_async_copy(sketch_hbm.at[t, 0], sk.at[t], load_sem.at[t]) for t in range(steps)
+        pltpu.make_async_copy(sketch_hbm.at[2 * p : 2 * p + 2, 0], sk.at[2 * p : 2 * p + 2], load_sem.at[p])
+        for p in range(pairs)
     ]
     kern_loads = [
-        pltpu.make_async_copy(kern_hbm.at[lag, 0], kv.at[lag], load_sem.at[steps + lag])
-        for lag in range(steps)
+        pltpu.make_async_copy(kern_hbm.at[lag : lag + 4, 0], kv.at[lag : lag + 4], load_sem.at[pairs + i])
+        for i, lag in enumerate(range(0, steps, 4))
     ]
     small_loads = [
-        pltpu.make_async_copy(src, dst, load_sem.at[2 * steps + i])
+        pltpu.make_async_copy(src, dst, load_sem.at[pairs + 2 + i])
         for i, (src, dst) in enumerate(
             ((couple_hbm, couple_ref), (diag_hbm, diag_ref), (prec_hbm, prec_ref))
         )
@@ -127,18 +142,21 @@
 
     def coef_copies(side, where):
         return [
-            remote(ref, coef_in.at[side, i], coef_send.at[side, i], coef_recv.at[side, i], where)
+            remote(ref, coef_in.at[side, i], coef_send.at[side], coef_recv.at[side], where)
             for i, ref in enumerate((couple_hbm, diag_hbm))
         ]
 
+    def coef_bulk(side, where):
+        return remote(coef_in.at[side], coef_in.at[side], coef_send.at[side], coef_recv.at[side], where)
+
     def halo_copy(f, side, where):
         return remote(
-            stage.at[f, 1 - side], hin.at[f, side], halo_send.at[f, side], halo_recv.at[f, side], where
+            stage.at[f, 1 - side], hin.at[f, side], halo_send.at[side], halo_recv.at[f, side], where
         )
 
     def edge_copy(f, side, where):
         return remote(
-            edge_out.at[f, 1 - side], edge_in.at[f, side], edge_send.at[f, side], edge_recv.at[f, side], where
+            edge_out.at[f, 1 - side], edge_in.at[f, side], edge_send.at[side], edge_recv.at[f, side], where
         )
 
     def send_halos(f, copy):
@@ -154,16 +172,26 @@
         @pl.when(has_up)
         def _():
             copy(f, 0, up).wait_recv()
-            copy(f, 1, up).wait_send()
 
         @pl.when(has_down)
         def _():
             copy(f, 1, down).wait_recv()
-            copy(f, 0, down).wait_send()
+
+    def halos_sent(source, send):
+        def one_side(side):
+            block = source.at[:, 1 - side]
+            remote(block, block, send.at[side], send.at[side], twin).wait_send()
+
+        @pl.when(has_up)
+        def _():
+            one_side(1)
+
+        @pl.when(has_down)
+        def _():
+            one_side(0)
 
     for p in range(pairs):
-        sketch_loads[2 * p].wait()
-        sketch_loads[2 * p + 1].wait()
+        sketch_loads[p].wait()
 
         for r in range(rows):
             first, second = sk[2 * p, r], sk[2 * p + 1, r]
@@ -239,26 +267,21 @@
             kt[lag, r * COLS : (r + 1) * COLS, :] = kv[lag, r].T
         return carry
 
-    for lag in range(steps // 2):
-        kern_loads[lag].wait()
+    kern_loads[0].wait()
     lax.fori_loop(0, steps // 2, flip, 0)
 
     @pl.when(has_up)
     def _():
-        for copy in coef_copies(0, up):
-            copy.wait_recv()
-        for copy in coef_copies(1, up):
-            copy.wait_send()
+        coef_bulk(0, up).wait_recv()
+        coef_bulk(1, up).wait_send()
         cpl[0] = over_lanes(coef_in[0, 0, rows - 2])
         cpl[1] = over_lanes(coef_in[0, 0, rows - 1])
         dia[0] = over_lanes(coef_in[0, 1, rows - 1])
 
     @pl.when(has_down)
     def _():
-        for copy in coef_copies(1, down):
-            copy.wait_recv()
-        for copy in coef_copies(0, down):
-            copy.wait_send()
+        coef_bulk(1, down).wait_recv()
+        coef_bulk(0, down).wait_send()
         cpl[rows + 2] = over_lanes(coef_in[1, 0, 0])
         cpl[rows + 3] = over_lanes(coef_in[1, 0, 1])
         dia[rows + 1] = over_lanes(coef_in[1, 1, 0])
@@ -296,7 +319,7 @@
 
     def pair_copy(c):
         return remote(
-            total.at[c, pl.ds(twin_half, half)], pair_in.at[c], pair_send.at[c], pair_recv.at[c], twin
+            total.at[c, pl.ds(twin_half, half)], pair_in.at[c], pair_send, pair_recv.at[c], twin
         )
 
     def lags_dot(lags, lhs, rhs):
@@ -318,8 +341,7 @@
         start = jnp.where(fresh, 0, 4)
 
         at_step(k, 1, rest_of_kernel)
-        at_step(k, 2, lambda: to_plane(0))
-        at_step(k, 5, lambda: to_z(0), lambda: to_plane(2))
+        at_step(k, 3, lambda: to_plane(0))
 
         @pl.when(fresh)
         def _():
@@ -329,8 +351,8 @@
 
             lax.fori_loop(2 * c, 2 * c + 2, per_field, 0)
 
-        at_step(k, 3, lambda: to_plane(1))
-        at_step(k, 5, lambda: to_z(1))
+        at_step(k, 4, lambda: to_plane(1))
+        at_step(k, 5, lambda: to_plane(2))
         first = 2 * q + 1 - start // 2
 
         def lhs(lag):
@@ -350,13 +372,13 @@
 
     def plane_copies(c):
         copies = []
-        for d in range(1, here.plane):
+        for d in here.plane_offsets():
             g, where = here.in_plane(d)
             copies.append(
                 remote(
                     xsend.at[c, pl.ds(pl.multiple_of(g * piece, piece), piece)],
                     xin.at[c, pl.ds((d - 1) * piece, piece)],
-                    x_send.at[c], x_recv.at[c], where,
+                    x_send, x_recv.at[c], where,
                 )
             )
         return copies
@@ -366,15 +388,15 @@
         return remote(block, block, send, recv, twin)
 
     def to_plane(c):
-        pair_copy(c).wait()
+        pair_copy(c).wait_recv()
         xsend[c] = (total[c, pl.ds(my_half, half)] + pair_in[c]).astype(BF16)
         for copy in plane_copies(c):
             copy.start()
 
     def z_copies(c):
         return [
-            remote(zsend.at[c], zin.at[c, d - 1], z_send.at[c, d], z_recv.at[c, d], here.along_z(d))
-            for d in range(1, here.nz)
+            remote(zsend.at[c], zin.at[c, d - 1], z_send, z_recv.at[c], here.along_z(d))
+            for d in here.z_offsets()
         ]
 
     def own_sum(c):
@@ -385,7 +407,7 @@
         return acc
 
     def to_z(c):
-        bulk(c, x_send.at[c], x_recv.at[c]).wait()
+        bulk(c, x_send, x_recv.at[c]).wait_recv()
         zsend[c] = own_sum(c).astype(BF16)
         for copy in z_copies(c):
             copy.start()
@@ -396,9 +418,9 @@
             remote(
                 wsend.at[c],
                 wgt.at[h, 0, pl.ds(2 * q, 2), pl.ds(my_sensors, piece)],
-                g_send.at[c], g_recv.at[c], here.in_plane(d)[1],
+                g_send, g_recv.at[c], here.in_plane(d)[1],
             )
-            for d in range(1, here.plane)
+            for d in here.plane_offsets()
         ]
 
     spot = lax.broadcasted_iota(jnp.int32, (piece, sensors), 1)
@@ -410,8 +432,7 @@
 
     def to_gather(c):
         h, q = c // 2, c % 2
-        for copy in z_copies(c):
-            copy.wait()
+        remote(zin.at[c], zin.at[c], z_send, z_recv.at[c], twin).wait_recv()
         acc = own_sum(c)
         for d in range(zothers):
             acc = acc + zin[c, d].astype(F32)
@@ -427,27 +448,36 @@
     def twin_copy(c):
         h, q = c // 2, c % 2
         block = wgt.at[h, 0, pl.ds(2 * q, 2), pl.ds(my_half, half)]
-        return remote(block, block, p_send.at[c], p_recv.at[c], twin)
+        return remote(block, block, p_send, p_recv.at[c], twin)
+
+    def shift_blocks(c, base):
+        h, q = c // 2, c % 2
+        for p in (2, 3, 4) if q else (1,):
+            for s in range(0, half, min(half, COLS)):
+                block = pl.ds(pl.multiple_of(base + s, piece), min(half, COLS))
+                mixed = jnp.where(
+                    low[: min(half, COLS)],
+                    wgt[h, 0, p, block, :].astype(F32),
+                    wgt[h, 0, p - 1, block, :].astype(F32),
+                )
+                wgt[h, 1, p, block, :] = turn(mixed).astype(BF16)
 
     def to_twin(c):
-        bulk(c, g_send.at[c], g_recv.at[c]).wait()
+        bulk(c, g_send, g_recv.at[c]).wait_recv()
         twin_copy(c).start()
+        shift_blocks(c, my_half)
 
     def weights_in(c):
-        h, q = c // 2, c % 2
-        twin_copy(c).wait()
-        for p in (2, 3, 4) if q else (1,):
-            for s in range(0, sensors, COLS):
-                block = slice(s, s + COLS)
-                mixed = jnp.where(low, wgt[h, 0, p, block, :].astype(F32), wgt[h, 0, p - 1, block, :].astype(F32))
-                wgt[h, 1, p, block, :] = turn(mixed).astype(BF16)
+        twin_copy(c).wait_recv()
+        shift_blocks(c, twin_half)
 
     def back(k, carry):
         h, i = k // 3, lax.rem(k, 3)
         q = jnp.where(i == 0, 1, 0)
         c = 2 * h + q
         start = jnp.where(i == 2, 4, 0)
-        at_step(k, 3, lambda: to_twin(2), lambda: to_twin(3), lambda: weights_in(2), lambda: weights_in(3))
+        at_step(k, 2, lambda: to_twin(2))
+        at_step(k, 3, lambda: to_twin(3), lambda: weights_in(2), lambda: weights_in(3))
         first = 2 * q + start // 2
 
         def lhs(lag):
@@ -471,57 +501,61 @@
         return carry
 
     def out_copy(t):
-        return pltpu.make_async_copy(sk.at[t], out_hbm.at[t, 0], out_sem.at[t])
+        return pltpu.make_async_copy(sk.at[t], out_hbm.at[t, 0], out_sem)
 
     def result(f):
         wait_halos(f, edge_copy)
         return rows_of(lambda r: adj[f, pl.ds(r * COLS, COLS), :], edge_in, f)
 
-    def first_half(k, carry):
+    def finish(k, carry):
         p = lax.rem(k + 2, pairs)
+        f = k // pairs * pairs + p
 
         def put(r, new):
-            field[p, r] = new
-
-        sweeps(result(p), put)
+            field[f, r] = new
+
+        sweeps(result(f), put)
+
+        @pl.when(k >= pairs)
+        def _():
+            for r in range(rows):
+                first, second = field[p, r], field[pairs + p, r]
+                crossed = turn(jnp.where(low, second, first))
+                sk[2 * p, r] = jnp.where(low, first, crossed)
+                sk[2 * p + 1, r] = jnp.where(low, crossed, second)
+            out_copy(2 * p).start()
+            out_copy(2 * p + 1).start()
+
         return carry
 
-    def second_half(k, carry):
-        p = lax.rem(k + 2, pairs)
-
-        def put(r, new):
-            before = field[p, r]
-            crossed = turn(jnp.where(low, new, before))
-            sk[2 * p, r] = jnp.where(low, before, crossed)
-            sk[2 * p + 1, r] = jnp.where(low, crossed, new)
-
-        sweeps(result(pairs + p), put)
-        out_copy(2 * p).start()
-        out_copy(2 * p + 1).start()
-        return carry
-
     def rest_of_kernel():
-        for lag in range(steps // 2, steps):
-            kern_loads[lag].wait()
+        kern_loads[1].wait()
 
     lax.fori_loop(0, 6, forward, 0)
+    to_z(0)
     to_plane(3)
+    to_z(1)
     lax.fori_loop(steps // 2, steps, flip, 0)
+    to_z(2)
     to_gather(0)
-    to_z(2)
     to_gather(1)
     to_z(3)
+    to_gather(2)
     to_twin(0)
-    to_gather(2)
+    to_gather(3)
     to_twin(1)
-    to_gather(3)
     weights_in(0)
     weights_in(1)
+    halos_sent(stage, halo_send)
+    remote(pair_in, pair_in, pair_send, pair_send, twin).wait_send()
+    remote(xin, xin, x_send, x_send, twin).wait_send()
+    remote(zin, zin, z_send, z_send, twin).wait_send()
     lax.fori_loop(0, 6, back, 0)
-    lax.fori_loop(0, pairs, first_half, 0)
-    lax.fori_loop(0, pairs, second_half, 0)
-    for t in range(steps):
-        out_copy(t).wait()
+    remote(xin, xin, g_send, g_send, twin).wait_send()
+    remote(xsend, xsend, p_send, p_send, twin).wait_send()
+    lax.fori_loop(0, steps, finish, 0)
+    halos_sent(edge_out, edge_send)
+    pltpu.make_async_copy(sk, out_hbm.at[:, 0], out_sem).wait()
 
 
 def split(mesh):
@@ -587,16 +621,16 @@
             pltpu.VMEM((rows + 4, cols, width), F32),
             pltpu.VMEM((rows + 2, cols, width), F32),
             *sweep_scratch,
-            dma((2 * steps + 3,)),
-            dma((2, 2)), dma((2, 2)),
-            dma((steps, 2)), dma((steps, 2)),
-            dma((chunks,)), dma((chunks,)),
-            dma((chunks,)), dma((chunks,)),
-            dma((chunks, nz)), dma((chunks, nz)),
-            dma((chunks,)), dma((chunks,)),
-            dma((chunks,)), dma((chunks,)),
-            dma((steps, 2)), dma((steps, 2)),
-            dma((steps,)),
+            dma((chunks + 5,)),
+            dma((2,)), dma((2,)),
+            dma((2,)), dma((steps, 2)),
+            dma(()), dma((chunks,)),
+            dma(()), dma((chunks,)),
+            dma(()), dma((chunks,)),
+            dma(()), dma((chunks,)),
+            dma(()), dma((chunks,)),
+            dma((2,)), dma((steps, 2)),
+            dma(()),
         ],
         compiler_params=pltpu.CompilerParams(
             collective_id=0, has_side_effects=True, vmem_limit_bytes=48 * 1024 * 1024

time: 62.1 us -> 60 us (0.966)
  Pallas kernels: 60 us -> 57.5 us
    pallas_call x1, Pallas kernels: 60 us -> 57.5 us  [body(): pl.pallas_call(functools.partial(main_kernel, sizes), out_shape=jax.Shape...]
where the time goes in v4:
time: 60 us; the launch traced here: 59.2 us
  Pallas kernels  57.5 us (96%)
  local copies, waits for them, and re-layouts  1.67 us (3%)
    pallas_call x1, Pallas kernels, body(): pl.pallas_call(functools.partial(main_kernel, sizes), out_shape=jax.Shape...  57.5 us
    unnamed x1, local copies, waits for them, and re-layouts  1.67 us

profile of v4, /device:TPU:16, one launch (start us, length us, event | category | flops | bytes accessed | tf_op | source)
XLA Modules:
  0.0 59.2 jit_solution(9669281791096079423)
XLA Ops:
  0.0 57.5 %sketch_main.1 = f32[8,1,6,128,128]{4,3,2,1,0:T(8,128)S(1)} custom-call(f32[8,1,6,128,128]{4,3,2,1,0:T(8,128)} %sketch_hbm.1, f32[6,1,128]{2,1,0:T(1,128)} %bitcast.4, f32[6,1,128]{2,1,0:T(1,128)} %bitcast.5, bf16[8,1,6,512,128]{4,3,2,1,0:T(8,128)(2,1)} %bitcast.3, f32[8,512]{1,0:T(8,128)} %prec_hbm.1), custom_call_target="tpu_custom_call" | custom-call | tf_op jit(solution)/shard_map/sketch_main/pallas_call | solution.py:593
  57.5 1.7 %copy.7 = f32[8,1,6,128,128]{4,3,2,1,0:T(8,128)} copy(f32[8,1,6,128,128]{4,3,2,1,0:T(8,128)S(1)} %sketch_main.1) | data formatting | bytes 6291456

commit v5 on v4

--- a/solution.py
+++ b/solution.py
@@ -268,7 +268,6 @@
         return carry
 
     kern_loads[0].wait()
-    lax.fori_loop(0, steps // 2, flip, 0)
 
     @pl.when(has_up)
     def _():
@@ -476,8 +475,8 @@
         q = jnp.where(i == 0, 1, 0)
         c = 2 * h + q
         start = jnp.where(i == 2, 4, 0)
-        at_step(k, 2, lambda: to_twin(2))
-        at_step(k, 3, lambda: to_twin(3), lambda: weights_in(2), lambda: weights_in(3))
+        at_step(k, 2, lambda: to_twin(2), lambda: to_twin(3))
+        at_step(k, 3, lambda: weights_in(2), lambda: weights_in(3))
         first = 2 * q + start // 2
 
         def lhs(lag):
@@ -534,12 +533,13 @@
     lax.fori_loop(0, 6, forward, 0)
     to_z(0)
     to_plane(3)
+    lax.fori_loop(0, steps // 2, flip, 0)
     to_z(1)
     lax.fori_loop(steps // 2, steps, flip, 0)
     to_z(2)
     to_gather(0)
+    to_z(3)
     to_gather(1)
-    to_z(3)
     to_gather(2)
     to_twin(0)
     to_gather(3)

time: 60 us -> 60.4 us (level)
  no operation moved by 1% of the time
where the time goes in v5:
time: 60.4 us; the launch traced here: 59.6 us
  Pallas kernels  57.9 us (96%)
  local copies, waits for them, and re-layouts  1.67 us (3%)
    pallas_call x1, Pallas kernels, body(): pl.pallas_call(functools.partial(main_kernel, sizes), out_shape=jax.Shape...  57.9 us
    unnamed x1, local copies, waits for them, and re-layouts  1.67 us

profile of v5, /device:TPU:16, one launch (start us, length us, event | category | flops | bytes accessed | tf_op | source)
XLA Modules:
  0.0 59.6 jit_solution(15967422545608742779)
XLA Ops:
  0.0 57.9 %sketch_main.1 = f32[8,1,6,128,128]{4,3,2,1,0:T(8,128)S(1)} custom-call(f32[8,1,6,128,128]{4,3,2,1,0:T(8,128)} %sketch_hbm.1, f32[6,1,128]{2,1,0:T(1,128)} %bitcast.4, f32[6,1,128]{2,1,0:T(1,128)} %bitcast.5, bf16[8,1,6,512,128]{4,3,2,1,0:T(8,128)(2,1)} %bitcast.3, f32[8,512]{1,0:T(8,128)} %prec_hbm.1), custom_call_target="tpu_custom_call" | custom-call | tf_op jit(solution)/shard_map/sketch_main/pallas_call | solution.py:593
  57.9 1.7 %copy.7 = f32[8,1,6,128,128]{4,3,2,1,0:T(8,128)} copy(f32[8,1,6,128,128]{4,3,2,1,0:T(8,128)S(1)} %sketch_main.1) | data formatting | bytes 6291456

commit v6 on v4

--- a/solution.py
+++ b/solution.py
@@ -268,7 +268,6 @@
         return carry
 
     kern_loads[0].wait()
-    lax.fori_loop(0, steps // 2, flip, 0)
 
     @pl.when(has_up)
     def _():
@@ -351,7 +350,7 @@
 
             lax.fori_loop(2 * c, 2 * c + 2, per_field, 0)
 
-        at_step(k, 4, lambda: to_plane(1))
+        at_step(k, 3, lambda: to_plane(1))
         at_step(k, 5, lambda: to_plane(2))
         first = 2 * q + 1 - start // 2
 
@@ -533,17 +532,17 @@
 
     lax.fori_loop(0, 6, forward, 0)
     to_z(0)
+    to_z(1)
     to_plane(3)
-    to_z(1)
-    lax.fori_loop(steps // 2, steps, flip, 0)
+    lax.fori_loop(0, steps, flip, 0)
     to_z(2)
     to_gather(0)
     to_gather(1)
     to_z(3)
     to_gather(2)
     to_twin(0)
+    to_twin(1)
     to_gather(3)
-    to_twin(1)
     weights_in(0)
     weights_in(1)
     halos_sent(stage, halo_send)

time: 60 us -> 59.1 us (0.985)
  Pallas kernels: 57.5 us -> 56.8 us
    pallas_call x1, Pallas kernels: 57.5 us -> 56.8 us  [body(): pl.pallas_call(functools.partial(main_kernel, sizes), out_shape=jax.Shape...]
where the time goes in v6:
time: 59.1 us; the launch traced here: 58.5 us
  Pallas kernels  56.8 us (96%)
  local copies, waits for them, and re-layouts  1.67 us (3%)
    pallas_call x1, Pallas kernels, body(): pl.pallas_call(functools.partial(main_kernel, sizes), out_shape=jax.Shape...  56.8 us
    unnamed x1, local copies, waits for them, and re-layouts  1.67 us

profile of v6, /device:TPU:16, one launch (start us, length us, event | category | flops | bytes accessed | tf_op | source)
XLA Modules:
  0.0 58.5 jit_solution(13784302543708837906)
XLA Ops:
  0.0 56.8 %sketch_main.1 = f32[8,1,6,128,128]{4,3,2,1,0:T(8,128)S(1)} custom-call(f32[8,1,6,128,128]{4,3,2,1,0:T(8,128)} %sketch_hbm.1, f32[6,1,128]{2,1,0:T(1,128)} %bitcast.4, f32[6,1,128]{2,1,0:T(1,128)} %bitcast.5, bf16[8,1,6,512,128]{4,3,2,1,0:T(8,128)(2,1)} %bitcast.3, f32[8,512]{1,0:T(8,128)} %prec_hbm.1), custom_call_target="tpu_custom_call" | custom-call | tf_op jit(solution)/shard_map/sketch_main/pallas_call | solution.py:592
  56.8 1.7 %copy.7 = f32[8,1,6,128,128]{4,3,2,1,0:T(8,128)} copy(f32[8,1,6,128,128]{4,3,2,1,0:T(8,128)S(1)} %sketch_main.1) | data formatting | bytes 6291456

commit v7 on v6

--- a/solution.py
+++ b/solution.py
@@ -90,12 +90,12 @@
 def main_kernel(
     sizes,
     sketch_hbm, diag_hbm, couple_hbm, kern_hbm, prec_hbm,
-    out_hbm,
+    out_ref,
     diag_ref, couple_ref, prec_ref,
     kv, kt, sk, field, stage, hin, smooth, total, pair_in, xsend, xin, zsend, zin, wsend, wgt, adj,
     edge_out, edge_in, coef_in, cpl, dia, coupled, again, swept,
     load_sem, coef_send, coef_recv, halo_send, halo_recv, pair_send, pair_recv, x_send, x_recv,
-    z_send, z_recv, g_send, g_recv, p_send, p_recv, edge_send, edge_recv, out_sem,
+    z_send, z_recv, g_send, g_recv, p_send, p_recv, edge_send, edge_recv,
 ):
     here = Place(sizes)
     steps, rows, sensors, _ = kv.shape
@@ -499,9 +499,6 @@
 
         return carry
 
-    def out_copy(t):
-        return pltpu.make_async_copy(sk.at[t], out_hbm.at[t, 0], out_sem)
-
     def result(f):
         wait_halos(f, edge_copy)
         return rows_of(lambda r: adj[f, pl.ds(r * COLS, COLS), :], edge_in, f)
@@ -520,10 +517,8 @@
             for r in range(rows):
                 first, second = field[p, r], field[pairs + p, r]
                 crossed = turn(jnp.where(low, second, first))
-                sk[2 * p, r] = jnp.where(low, first, crossed)
-                sk[2 * p + 1, r] = jnp.where(low, crossed, second)
-            out_copy(2 * p).start()
-            out_copy(2 * p + 1).start()
+                out_ref[2 * p, 0, r] = jnp.where(low, first, crossed)
+                out_ref[2 * p + 1, 0, r] = jnp.where(low, crossed, second)
 
         return carry
 
@@ -554,7 +549,6 @@
     remote(xsend, xsend, p_send, p_send, twin).wait_send()
     lax.fori_loop(0, steps, finish, 0)
     halos_sent(edge_out, edge_send)
-    pltpu.make_async_copy(sk, out_hbm.at[:, 0], out_sem).wait()
 
 
 def split(mesh):
@@ -593,7 +587,7 @@
         functools.partial(main_kernel, sizes),
         out_shape=jax.ShapeDtypeStruct(sketch.shape, F32),
         in_specs=[pl.BlockSpec(memory_space=pltpu.HBM)] * 5,
-        out_specs=anywhere,
+        out_specs=pl.BlockSpec(memory_space=pltpu.VMEM),
         scratch_shapes=[
             pltpu.VMEM(diag_rows.shape, F32),
             pltpu.VMEM(couple_rows.shape, F32),
@@ -629,7 +623,6 @@
             dma(()), dma((chunks,)),
             dma(()), dma((chunks,)),
             dma((2,)), dma((steps, 2)),
-            dma(()),
         ],
         compiler_params=pltpu.CompilerParams(
             collective_id=0, has_side_effects=True, vmem_limit_bytes=48 * 1024 * 1024

time: 59.1 us -> 58.8 us (level)
  no operation moved by 1% of the time
where the time goes in v7:
time: 58.8 us; the launch traced here: 58.1 us
  Pallas kernels  56.4 us (96%)
  local copies, waits for them, and re-layouts  1.67 us (3%)
    pallas_call x1, Pallas kernels, body(): pl.pallas_call(functools.partial(main_kernel, sizes), out_shape=jax.Shape...  56.4 us
    unnamed x1, local copies, waits for them, and re-layouts  1.67 us

profile of v7, /device:TPU:16, one launch (start us, length us, event | category | flops | bytes accessed | tf_op | source)
XLA Modules:
  0.0 58.1 jit_solution(13002439018651058012)
XLA Ops:
  0.0 56.4 %sketch_main.1 = f32[8,1,6,128,128]{4,3,2,1,0:T(8,128)S(1)} custom-call(f32[8,1,6,128,128]{4,3,2,1,0:T(8,128)} %sketch_hbm.1, f32[6,1,128]{2,1,0:T(1,128)} %bitcast.4, f32[6,1,128]{2,1,0:T(1,128)} %bitcast.5, bf16[8,1,6,512,128]{4,3,2,1,0:T(8,128)(2,1)} %bitcast.3, f32[8,512]{1,0:T(8,128)} %prec_hbm.1), custom_call_target="tpu_custom_call" | custom-call | tf_op jit(solution)/shard_map/sketch_main/pallas_call | solution.py:586
  56.4 1.7 %copy.7 = f32[8,1,6,128,128]{4,3,2,1,0:T(8,128)} copy(f32[8,1,6,128,128]{4,3,2,1,0:T(8,128)S(1)} %sketch_main.1) | data formatting | bytes 6291456

commit v8 on v7

--- a/solution.py
+++ b/solution.py
@@ -351,7 +351,7 @@
             lax.fori_loop(2 * c, 2 * c + 2, per_field, 0)
 
         at_step(k, 3, lambda: to_plane(1))
-        at_step(k, 5, lambda: to_plane(2))
+        at_step(k, 5, lambda: to_plane(2), lambda: to_z(0))
         first = 2 * q + 1 - start // 2
 
         def lhs(lag):
@@ -526,7 +526,6 @@
         kern_loads[1].wait()
 
     lax.fori_loop(0, 6, forward, 0)
-    to_z(0)
     to_z(1)
     to_plane(3)
     lax.fori_loop(0, steps, flip, 0)

time: 58.8 us -> 58.8 us (level)
  no operation moved by 1% of the time
where the time goes in v8:
time: 58.8 us; the launch traced here: 58.2 us
  Pallas kernels  56.6 us (96%)
  local copies, waits for them, and re-layouts  1.67 us (3%)
    pallas_call x1, Pallas kernels, body(): pl.pallas_call(functools.partial(main_kernel, sizes), out_shape=jax.Shape...  56.6 us
    unnamed x1, local copies, waits for them, and re-layouts  1.67 us

profile of v8, /device:TPU:16, one launch (start us, length us, event | category | flops | bytes accessed | tf_op | source)
XLA Modules:
  0.0 58.2 jit_solution(3756648286868972038)
XLA Ops:
  0.0 56.6 %sketch_main.1 = f32[8,1,6,128,128]{4,3,2,1,0:T(8,128)S(1)} custom-call(f32[8,1,6,128,128]{4,3,2,1,0:T(8,128)} %sketch_hbm.1, f32[6,1,128]{2,1,0:T(1,128)} %bitcast.4, f32[6,1,128]{2,1,0:T(1,128)} %bitcast.5, bf16[8,1,6,512,128]{4,3,2,1,0:T(8,128)(2,1)} %bitcast.3, f32[8,512]{1,0:T(8,128)} %prec_hbm.1), custom_call_target="tpu_custom_call" | custom-call | tf_op jit(solution)/shard_map/sketch_main/pallas_call | solution.py:585
  56.6 1.7 %copy.7 = f32[8,1,6,128,128]{4,3,2,1,0:T(8,128)} copy(f32[8,1,6,128,128]{4,3,2,1,0:T(8,128)S(1)} %sketch_main.1) | data formatting | bytes 6291456
